TPU v7x, 128 devices: a whole 4x4x4 slice. The times are simulated.
128 devices in a mesh: mode: 32 (over z, y, core), slab: 4 (over x).
Axes of the slice: x: 4, y: 4, z: 4, core: 2. Of those that a mesh axis runs over, the one named last changes fastest.
Arguments:
- guess: float32 [4096, 128, 128], P('mode', 'slab'), may hold values from -6 to 6
- right_side: float32 [4096, 128, 128], P('mode', 'slab'), may hold values from -6 to 6
- mean_coef: float32 [128, 128], P('slab'), may hold values from 0.5 to 2
- field_coef: float32 [3, 128, 128], P(None, 'slab'), may hold values from -2.5 to 2.5
- coupling: bfloat16 [32, 16, 128, 128], replicated, may hold values from -0.0625 to 0.0625
- coupling_list: int32 [32, 16], replicated, may hold values from 0 to 95, as said below
- pair_count: int32 [32], replicated, may hold values from 4 to 16, as said below
Outputs:
- solution: float32 [4096, 128, 128], P('mode', 'slab')
- residual: float32 [4096, 128, 128], P('mode', 'slab')
Inputs may be any that keep to these rules, and one draw needn't show every extreme that they name: `coupling_list`: each row holds 16 distinct entries; entry e couples its row's mode block to mode block e // 3 through coefficient field e % 3. Only the first pair_count entries of a row are live. `pair_count`: number of live entries of each mode block's row.
All inputs are finite; a program needn't handle non-finite values.
Results may differ from a plain program's by a relative error of at most 0.0012.
Values may be sent and summed in bfloat16 or wider, within the bound.
A program may use at most 256 MiB of HBM per device.

v0:
```python
import math

import jax
import jax.numpy as jnp
from jax import lax
from jax.sharding import PartitionSpec as P

FIELDS = 3
MAXC = 16
NX = 128
NY = 128
ITERS = 2


relaxation = 0.6


def with_halo(block, sides, width):
    for axis, dim in sides:
        count = lax.axis_size(axis)
        forward = [(i, i + 1) for i in range(count - 1)]
        backward = [(target, source) for source, target in forward]
        low = lax.ppermute(
            lax.slice_in_dim(block, block.shape[dim] - width, None, axis=dim), axis, forward
        )
        high = lax.ppermute(lax.slice_in_dim(block, 0, width, axis=dim), axis, backward)
        block = jnp.concatenate([low, block, high], axis=dim)
    return block


def in_blocks(array, dim, size):
    lengths = array.shape
    blocks = array.reshape(*lengths[:dim], size, lengths[dim] // size, *lengths[dim + 1 :])
    return jnp.moveaxis(blocks, dim, 0)


def piece_ends(length, count):
    unit = 8 if length >= 8 * count else 1
    return [length // unit * k // count * unit for k in range(1, count)]


def laid_out(blocks, dim):
    lengths = list(blocks.shape[1:])
    lengths[dim] *= blocks.shape[0]
    return jnp.moveaxis(blocks, 0, dim).reshape(lengths)


def cut_exchange(array, axis, pieces, split_dim, concat_dim):
    blocks = in_blocks(array, split_dim, lax.axis_size(axis))
    cut = max(range(1, max(2, blocks.ndim - 1)), key=lambda d: blocks.shape[d])
    finished = []
    for slab in jnp.split(blocks, piece_ends(blocks.shape[cut], pieces), axis=cut):
        if slab.size:
            finished.append(lax.all_to_all(slab, axis, split_axis=0, concat_axis=0, tiled=True))
    return laid_out(jnp.concatenate(finished, axis=cut), concat_dim)


def operate(padded, coef_pad):
    center = coef_pad[..., 1:-1, :]
    field = padded[..., 1:-1, :]
    result = 0.5 * (center + coef_pad[..., :-2, :]) * (field - padded[..., :-2, :])
    result = result + 0.5 * (center + coef_pad[..., 2:, :]) * (field - padded[..., 2:, :])
    side_coef = jnp.pad(center, [(0, 0)] * (center.ndim - 1) + [(1, 1)], mode="edge")
    side_field = jnp.pad(field, [(0, 0)] * (field.ndim - 1) + [(1, 1)])
    result = result + 0.5 * (center + side_coef[..., :-2]) * (field - side_field[..., :-2])
    result = result + 0.5 * (center + side_coef[..., 2:]) * (field - side_field[..., 2:])
    return result


def sine_table(length):
    counter = jnp.arange(length).astype(jnp.float32) + 1.0
    angle = math.pi * counter[:, None] * counter[None, :] / (length + 1)
    return math.sqrt(2.0 / (length + 1)) * jnp.sin(angle)


def eigen_table(first, second):
    along_first = 2.0 * jnp.cos(
        math.pi * (jnp.arange(first).astype(jnp.float32) + 1.0) / (first + 1)
    )
    along_second = 2.0 * jnp.cos(
        math.pi * (jnp.arange(second).astype(jnp.float32) + 1.0) / (second + 1)
    )
    return 4.0 - along_first[:, None] - along_second[None, :]


def whole_solve(whole):
    highest = lax.Precision.HIGHEST
    rows_table = sine_table(NX)
    cols_table = sine_table(NY)
    spectral = jnp.einsum("px,mxy->mpy", rows_table, whole, precision=highest)
    spectral = jnp.einsum("mpy,yq->mpq", spectral, cols_table, precision=highest)
    spectral = spectral / eigen_table(NX, NY)
    spatial = jnp.einsum("xp,mpq->mxq", rows_table, spectral, precision=highest)
    return jnp.einsum("mxq,qy->mxy", spatial, cols_table, precision=highest)


def mean_solve(resid):
    whole = lax.all_to_all(resid, "slab", split_axis=0, concat_axis=1, tiled=True)
    spatial = whole_solve(whole)
    return lax.all_to_all(spatial, "slab", split_axis=1, concat_axis=0, tiled=True)


def local(guess, right_side, mean_coef, field_coef, coupling, coupling_list, pair_count):
    highest = lax.Precision.HIGHEST
    modes_dev, rows, cols = guess.shape
    blocks = coupling.shape[0]
    coefs = jnp.concatenate([mean_coef[None], field_coef], 0)
    partner = coupling_list // FIELDS
    field_index = coupling_list % FIELDS
    live_mask = jnp.arange(MAXC)[None, :] < pair_count[:, None]
    coef_halo = with_halo(coefs, (("slab", 1),), 1)
    at_top = lax.axis_index("slab") == 0
    at_bottom = lax.axis_index("slab") == lax.axis_size("slab") - 1
    upper = jnp.where(at_top, coefs[:, :1], coef_halo[:, :1])
    lower = jnp.where(at_bottom, coefs[:, -1:], coef_halo[:, -1:])
    coef_rows = jnp.concatenate([upper, coefs, lower], 1)
    field_rows = coef_rows[1:, None]
    solution = guess
    residual = right_side
    for sweep in range(ITERS):
        state_pad = with_halo(solution, (("slab", 1),), 1)
        mean_part = operate(state_pad, coef_rows[0])
        rounded = lax.optimization_barrier(state_pad.astype(jnp.bfloat16)).astype(jnp.float32)
        images = operate(rounded[None], field_rows)
        images = images.reshape(FIELDS, modes_dev, rows * cols)
        strip_images = cut_exchange(images, "mode", 2, 2, 1)
        strip_images = strip_images.reshape(FIELDS, blocks, modes_dev, -1)
        gathered = strip_images[field_index, partner] * live_mask[:, :, None, None].astype(
            jnp.float32
        )
        strip_sum = jnp.einsum(
            "ikab,ikbc->iac", coupling.astype(jnp.float32), gathered, precision=highest
        )
        strip_sum = strip_sum.reshape(blocks * modes_dev, -1)
        owner_sum = cut_exchange(strip_sum, "mode", 2, 0, 1)
        coupled = owner_sum.reshape(modes_dev, rows, cols)
        residual = right_side - mean_part - coupled
        solution = solution + relaxation * mean_solve(residual)
    return (solution, residual)


def solution(mesh):
    placed = (
        P("mode", "slab", None),
        P("mode", "slab", None),
        P("slab", None),
        P(None, "slab", None),
        P(),
        P(),
        P(),
    )
    return jax.shard_map(
        local,
        mesh=mesh,
        in_specs=placed,
        out_specs=(P("mode", "slab", None), P("mode", "slab", None)),
        check_vma=False,
    )
```

profile of v0, /device:TPU:1, one launch (start us, length us, event | category | flops | bytes accessed | tf_op | source)
XLA Modules:
  0.0 588.8 jit_solution(1291534412321245910)
XLA Ops:
  1.3 3.9 collective-permute-start
  5.3 4.3 copy.132
  9.6 1.3 collective-permute-start.2
  10.9 1.5 fusion.160
  12.4 4.0 collective-permute-start.1
  18.5 3.2 collective-permute-done.3
  30.3 2.9 multiply_add_fusion.1
  33.3 2.5 fusion.156
  35.8 50.3 %all_to_all.94 = f32[32,3,64,128]{3,2,1,0:T(8,128)S(1)} all-to-all(f32[32,3,64,128]{3,2,1,0:T(8,128)S(1)} %get-tuple-element.16), channel_id=1, replica_groups=mesh['mode'=32,'slab'=4] {'mode'}, dimensions={0} | all-to-all | bytes 6291456 | tf_op jit(solution)/shard_map/all_to_all | solution.py:54
  86.1 4.9 all-to-all-start.1
  91.3 39.7 %all-to-all-done.1 = f32[32,3,64,128]{3,2,1,0:T(8,128)} async-done(((f32[32,3,64,128]{3,2,1,0:T(8,128)}), f32[32,3,64,128]{3,2,1,0:T(8,128)}, u32[]{:S(2)}, u32[]{:S(2)}) %all-to-all-start.1) | async-done | bytes 3145760 | tf_op jit(solution)/shard_map/all_to_all | solution.py:54
  131.0 5.1 maximum_bitcast_fusion
  136.1 18.6 %gather_fusion = f32[512,128,128]{2,1,0:T(8,128)} fusion(f32[3,32,128,128]{3,2,0,1:T(8,128)} %maximum_bitcast_fusion, s32[512]{0:T(512)S(1)} %reshape.94), kind=kCustom, calls=%fused_computation | custom fusion | bytes 67112960 | tf_op jit(solution)/shard_map/gather | solution.py:128
  154.7 26.2 %fusion.58 = f32[32,128,128]{2,1,0:T(8,128)S(1)} fusion(bf16[32,16,128,128]{3,2,1,0:T(8,128)(2,1)} %param.11, f32[32,16,128,128]{3,2,1,0:T(8,128)} %bitcast.138, f32[32,16]{1,0:T(8,128)S(1)} %fusion.131), kind=kOutput, calls=%fused_computation.80 | convolution fusion | flops 12893290496 | bytes 52430848 | tf_op jit(solution)/shard_map/ikab,ikbc->iac/dot_general | solution.py:131
  182.1 22.4 %all_to_all.95 = f32[32,64,128]{2,1,0:T(8,128)S(1)} all-to-all(f32[32,64,128]{2,1,0:T(8,128)S(1)} %get-tuple-element.30), channel_id=1, replica_groups=mesh['mode'=32,'slab'=4] {'mode'}, dimensions={0} | all-to-all | bytes 2097152 | tf_op jit(solution)/shard_map/all_to_all | solution.py:54
  204.6 4.6 all-to-all-start.3
  210.0 16.4 %all-to-all-done.3 = f32[32,64,128]{2,1,0:T(8,128)} async-done(((f32[32,64,128]{2,1,0:T(8,128)}), f32[32,64,128]{2,1,0:T(8,128)}, u32[]{:S(2)}, u32[]{:S(2)}) %all-to-all-start.3) | async-done | bytes 1048608 | tf_op jit(solution)/shard_map/all_to_all | solution.py:54
  226.4 4.0 fusion.11
  230.4 2.5 copy.124
  232.9 4.1 all-to-all-start.4
  237.2 25.6 %all-to-all-done.4 = f32[128,32,128]{2,1,0:T(8,128)S(1)} async-done(((f32[128,32,128]{2,1,0:T(8,128)}), f32[128,32,128]{2,1,0:T(8,128)S(1)}, u32[]{:S(2)}, u32[]{:S(2)}) %all-to-all-start.4) | async-done | bytes 2097184 | tf_op jit(solution)/shard_map/all_to_all | solution.py:98
  262.9 3.6 fusion.76
  266.6 3.6 fusion.46
  270.2 5.0 fusion.52
  275.2 2.4 copy.148
  277.6 2.1 fusion.72
  279.7 27.1 %all_to_all.96 = f32[32,128,128]{2,0,1:T(8,128)S(1)} all-to-all(f32[32,128,128]{2,0,1:T(8,128)S(1)} %fusion.72), channel_id=1, replica_groups=mesh['mode'=32,'slab'=4] {'slab'}, dimensions={1} | all-to-all | bytes 4194304 | tf_op jit(solution)/shard_map/all_to_all | solution.py:100
  307.3 1.4 copy-done.1
  308.7 1.3 fusion.154
  310.0 2.2 collective-permute-start.4
  313.5 3.7 collective-permute-done.5
  319.5 2.9 multiply_add_fusion
  323.6 48.0 %all_to_all.97 = f32[32,3,64,128]{3,2,1,0:T(8,128)S(1)} all-to-all(f32[32,3,64,128]{3,2,1,0:T(8,128)S(1)} %get-tuple-element.14), channel_id=1, replica_groups=mesh['mode'=32,'slab'=4] {'mode'}, dimensions={0} | all-to-all | bytes 6291456 | tf_op jit(solution)/shard_map/all_to_all | solution.py:54
  371.6 43.4 %all_to_all.98 = f32[32,3,64,128]{3,2,1,0:T(8,128)S(1)} all-to-all(f32[32,3,64,128]{3,2,1,0:T(8,128)S(1)} %get-tuple-element.15), channel_id=1, replica_groups=mesh['mode'=32,'slab'=4] {'mode'}, dimensions={0} | all-to-all | bytes 6291456 | tf_op jit(solution)/shard_map/all_to_all | solution.py:54
  415.0 3.0 maximum_bitcast_fusion.1
  418.0 18.6 %gather_fusion.1 = f32[512,128,128]{2,1,0:T(8,128)} fusion(f32[3,32,128,128]{3,2,0,1:T(8,128)} %maximum_bitcast_fusion.1, s32[512]{0:T(512)S(1)} %reshape.94), kind=kCustom, calls=%fused_computation.1 | custom fusion | bytes 67112960 | tf_op jit(solution)/shard_map/gather | solution.py:128
  436.6 26.2 %fusion.61 = f32[32,128,128]{2,1,0:T(8,128)S(1)} fusion(bf16[32,16,128,128]{3,2,1,0:T(8,128)(2,1)} %param.11, f32[32,16,128,128]{3,2,1,0:T(8,128)} %bitcast.137, f32[32,16]{1,0:T(8,128)S(1)} %fusion.131), kind=kOutput, calls=%fused_computation.81 | convolution fusion | flops 12893290496 | bytes 52430848 | tf_op jit(solution)/shard_map/ikab,ikbc->iac/dot_general | solution.py:131
  463.2 20.7 %all_to_all.99 = f32[32,64,128]{2,1,0:T(8,128)S(1)} all-to-all(f32[32,64,128]{2,1,0:T(8,128)S(1)} %get-tuple-element.24), channel_id=1, replica_groups=mesh['mode'=32,'slab'=4] {'mode'}, dimensions={0} | all-to-all | bytes 2097152 | tf_op jit(solution)/shard_map/all_to_all | solution.py:54
  483.9 20.6 %all_to_all.100 = f32[32,64,128]{2,1,0:T(8,128)S(1)} all-to-all(f32[32,64,128]{2,1,0:T(8,128)S(1)} %get-tuple-element.25), channel_id=1, replica_groups=mesh['mode'=32,'slab'=4] {'mode'}, dimensions={0} | all-to-all | bytes 2097152 | tf_op jit(solution)/shard_map/all_to_all | solution.py:54
  504.6 3.9 fusion.23
  509.7 28.5 %all_to_all.101 = f32[128,32,128]{2,1,0:T(8,128)S(1)} all-to-all(f32[128,32,128]{2,1,0:T(8,128)S(1)} %copy.134), channel_id=1, replica_groups=mesh['mode'=32,'slab'=4] {'slab'}, dimensions={0} | all-to-all | bytes 4194304 | tf_op jit(solution)/shard_map/all_to_all | solution.py:98
  538.5 3.6 fusion.70
  542.1 3.6 fusion.44
  545.7 5.0 fusion.55
  550.7 3.4 copy.154
  554.1 3.7 fusion.66
  557.8 27.1 %all_to_all.102 = f32[32,128,128]{2,0,1:T(8,128)S(1)} all-to-all(f32[32,128,128]{2,0,1:T(8,128)S(1)} %fusion.66), channel_id=1, replica_groups=mesh['mode'=32,'slab'=4] {'slab'}, dimensions={1} | all-to-all | bytes 4194304 | tf_op jit(solution)/shard_map/all_to_all | solution.py:100
  585.7 2.5 copy.142
  (79 shorter events, 21.4 us)
Async XLA Ops:
  1.3 8.3 %collective-permute-start = (f32[4,1,128]{2,1,0:T(1,128)S(1)}, f32[4,1,128]{2,1,0:T(1,128)S(1)}, u32[]{:S(2)}, u32[]{:S(2)}) collective-permute-start(f32[4,1,128]{2,1,0:T(1,128)S(1)} %pad_maximum_fusion.17), channel_id=1, source_target_pairs={{0,1},{1,2},{2,3},{4,5},{5,6},{6,7},{8,9},{9,10},{10,11},{12,13},{... | collective-permute-start | bytes 6152 | tf_op jit(solution)/shard_map/ppermute | solution.py:23
  5.3 4.3 copy-start.5
  5.3 4.3 copy-start.6
  5.3 12.4 %copy-start = (f32[128,32,128]{2,1,0:T(8,128)S(1)}, f32[128,32,128]{2,1,0:T(8,128)}, u32[]{:S(2)}) copy-start(f32[128,32,128]{2,1,0:T(8,128)} %param.7) | copy-start | bytes 6291460
  9.6 8.4 %collective-permute-start.2 = (f32[4,1,128]{2,1,0:T(1,128)S(1)}, f32[4,1,128]{2,1,0:T(1,128)S(1)}, u32[]{:S(2)}, u32[]{:S(2)}) collective-permute-start(f32[4,1,128]{2,1,0:T(1,128)S(1)} %get-tuple-element.13), channel_id=1, source_target_pairs={{1,0},{2,1},{3,2},{5,4},{6,5},{7,6},{9,8},{10,9},{11,10},{13,12},{... | collective-permute-start | bytes 6152 | tf_op jit(solution)/shard_map/ppermute | solution.py:26
  12.4 6.0 %collective-permute-start.1 = (f32[128,1,128]{2,0,1:T(8,128)}, f32[128,1,128]{2,0,1:T(8,128)S(1)}, u32[]{:S(2)}, u32[]{:S(2)}) collective-permute-start(f32[128,1,128]{2,0,1:T(8,128)} %get-tuple-element.34), channel_id=1, source_target_pairs={{0,1},{1,2},{2,3},{4,5},{5,6},{6,7},{8,9},{9,10},{10,11},{12,13},{... | collective-permute-start | bytes 196616 | tf_op jit(solution)/shard_map/ppermute | solution.py:23
  16.4 5.3 collective-permute-start.3
  18.4 5.2 copy-start.7
  86.1 5.0 copy-start.9
  86.1 5.1 copy-start.10
  86.1 44.9 %all-to-all-start.1 = ((f32[32,3,64,128]{3,2,1,0:T(8,128)}), f32[32,3,64,128]{3,2,1,0:T(8,128)}, u32[]{:S(2)}, u32[]{:S(2)}) async-start(f32[32,3,64,128]{3,2,1,0:T(8,128)} %get-tuple-element.17), calls=%async_computation.1 | async-start | bytes 6291456 | tf_op jit(solution)/shard_map/all_to_all | solution.py:54
  182.1 44.3 %copy-start.2 = (f32[128,32,128]{2,0,1:T(8,128)S(1)}, f32[128,32,128]{2,0,1:T(8,128)}, u32[]{:S(2)}) copy-start(f32[128,32,128]{2,0,1:T(8,128)} %copy.132) | copy-start | bytes 6291460
  204.6 21.9 %all-to-all-start.3 = ((f32[32,64,128]{2,1,0:T(8,128)}), f32[32,64,128]{2,1,0:T(8,128)}, u32[]{:S(2)}, u32[]{:S(2)}) async-start(f32[32,64,128]{2,1,0:T(8,128)} %get-tuple-element.31), calls=%async_computation.3 | async-start | bytes 2097152 | tf_op jit(solution)/shard_map/all_to_all | solution.py:54
  232.9 29.9 %all-to-all-start.4 = ((f32[128,32,128]{2,1,0:T(8,128)}), f32[128,32,128]{2,1,0:T(8,128)S(1)}, u32[]{:S(2)}, u32[]{:S(2)}) async-start(f32[128,32,128]{2,1,0:T(8,128)} %copy.124), calls=%async_computation.4 | async-start | bytes 4194304 | tf_op jit(solution)/shard_map/all_to_all | solution.py:98
  307.1 1.6 copy-start.1
  310.0 3.5 collective-permute-start.4
  312.2 5.0 collective-permute-start.5
  463.1 41.4 %copy-start.4 = (f32[128,32,128]{2,1,0:T(8,128)S(1)}, f32[128,32,128]{2,1,0:T(8,128)}, u32[]{:S(2)}) copy-start(f32[128,32,128]{2,1,0:T(8,128)} %param.8) | copy-start | bytes 6291460
  463.2 41.4 %copy-start.8 = (f32[32,128]{1,0:T(8,128)S(1)}, f32[32,128]{1,0:T(8,128)}, u32[]{:S(2)}) copy-start(f32[32,128]{1,0:T(8,128)} %get-tuple-element.37) | copy-start | bytes 49156
  509.7 28.6 %copy-start.3 = (f32[128,32,128]{2,1,0:T(8,128)}, f32[128,32,128]{2,1,0:T(8,128)S(1)}, u32[]{:S(2)}) copy-start(f32[128,32,128]{2,1,0:T(8,128)S(1)} %copy.134) | copy-start | bytes 6291460
where the time goes:
time: 600 us; the launch traced here: 589 us
  blocking collectives  288 us (48%)
  waiting for transfers between devices  88.6 us (15%)
  matrix products  82.8 us (14%)
  local copies, waits for them, and re-layouts  67.9 us (11%)
  other arithmetic  31.9 us (5%)
  starting transfers between devices  27.7 us (5%)
    all_to_all x6, blocking collectives, cut_exchange(): lax.all_to_all(slab, axis, split_axis=0, concat_axis=0, tiled=True)  205 us
    all_to_all x2, waiting for transfers between devices, cut_exchange(): lax.all_to_all(slab, axis, split_axis=0, concat_axis=0, tiled=True)  56.1 us
    all_to_all x2, blocking collectives, mean_solve(): lax.all_to_all(spatial, 'slab', split_axis=1, concat_axis=0, tiled=True)  54.2 us
    dot_general x2, matrix products, local(): jnp.einsum('ikab,ikbc->iac', coupling.astype(jnp.float32), gathered, prec...  52.5 us
    gather x2, local copies, waits for them, and re-layouts, local(): strip_images[field_index, partner]  37.2 us
    all_to_all x1, blocking collectives, mean_solve(): lax.all_to_all(resid, 'slab', split_axis=0, concat_axis=1, tiled=True)  28.5 us
    all_to_all x1, waiting for transfers between devices, mean_solve(): lax.all_to_all(resid, 'slab', split_axis=0, concat_axis=1, tiled=True)  25.6 us
  transfers between devices with their start and end apart: 9, of which 5 were waited for; matrix products, arithmetic and copies ran while one was open for 1% of the time, Pallas kernels for 0%

commit v1 on v0

v1 whole, which is shorter than its diff:
```python
import functools
import math

import jax
import jax.numpy as jnp
import numpy as np
from jax import lax
from jax.experimental import pallas as pl
from jax.experimental.pallas import tpu as pltpu
from jax.sharding import PartitionSpec as P

FIELDS = 3
MAXC = 16
BLK = 128
ITERS = 2
RELAX = 0.6
F32 = jnp.float32
BF16 = jnp.bfloat16


LOW_ROWS = 8
LOW_COLS = 16


def halves(table):
    hi = np.asarray(table, np.float32).astype(BF16)
    lo = (np.asarray(table, np.float32) - hi.astype(np.float32)).astype(BF16)
    return hi, lo, np.zeros_like(hi)


def fore_table(sine):
    hi, lo, zero = halves(sine)
    low = np.tile(hi[:, :LOW_COLS], (1, LOW_ROWS))
    return np.concatenate(
        [np.concatenate([hi, lo, low], 1), np.concatenate([hi, zero, zero], 1)], 0
    )


def back_table(sine):
    hi, lo, zero = halves(sine)
    low = np.tile(hi[:LOW_COLS], (LOW_ROWS, 1))
    return np.concatenate(
        [
            np.concatenate([hi, lo], 1),
            np.concatenate([hi, zero], 1),
            np.concatenate([low, zero], 1),
        ],
        0,
    )


def single(length):
    f32 = np.float32
    counter = np.arange(length).astype(f32) + f32(1.0)
    angle = f32(math.pi) * counter[:, None] * counter[None] / f32(length + 1)
    sine = np.sin(angle.astype(np.float64)).astype(f32)
    sine = f32(math.sqrt(2.0 / (length + 1))) * sine
    turn = f32(math.pi) * counter / f32(length + 1)
    return sine, f32(2.0) * np.cos(turn.astype(np.float64)).astype(f32)


def tables(rows, cols, slabs):
    length = rows * slabs
    sine, along = single(cols)
    across = single(length)[1]
    diag = 4.0 - along.astype(np.float64)
    pivot = np.zeros((rows, cols))
    pivot[0] = 1.0 / diag
    for x in range(1, rows):
        pivot[x] = 1.0 / (diag - pivot[x - 1])
    reach = np.cumprod(pivot, axis=0)
    first = np.zeros((rows, cols))
    meet = np.zeros((slabs, 2, 2 * slabs, cols))
    eye = np.eye(rows)
    shift = np.eye(rows, k=1) + np.eye(rows, k=-1)
    for q in range(cols):
        column = np.linalg.solve(diag[q] * eye - shift, eye[0])
        first[:, q] = column
        near, far = column[0], column[-1]
        system = np.eye(2 * slabs)
        for s in range(slabs):
            if s > 0:
                system[s, slabs + s - 1] -= near
                system[slabs + s, slabs + s - 1] -= far
            if s < slabs - 1:
                system[s, s + 1] -= far
                system[slabs + s, s + 1] -= near
        inverse = np.linalg.inv(system)
        for s in range(slabs):
            if s > 0:
                meet[s, 0, :, q] = inverse[slabs + s - 1]
            if s < slabs - 1:
                meet[s, 1, :, q] = inverse[s + 1]
    p = np.arange(LOW_ROWS)
    rounded = (np.float32(4.0) - across[:LOW_ROWS, None]) - along[None, :LOW_COLS]
    smooth = diag[None, :LOW_COLS] - 2.0 * np.cos(np.pi * (p + 1.0) / (length + 1))[:, None]
    gap = 1.0 / rounded.astype(np.float64) - 1.0 / smooth
    gap = np.broadcast_to(gap.reshape(1, cols), (8, cols)).astype(np.float32)
    place = np.arange(slabs)[:, None] * rows + np.arange(rows + 2)[None]
    waves = np.sqrt(2.0 / (length + 1)) * np.sin(
        np.pi * place[:, :, None] * (p + 1.0) / (length + 1)
    )
    waves = np.repeat(waves, LOW_COLS, axis=2)
    waves = np.broadcast_to(waves[:, :, None], (slabs, rows + 2, 8, cols)).astype(np.float32)
    sweep = np.stack([pivot, first, reach])
    sweep = np.broadcast_to(sweep[:, :, None], (3, rows, 8, cols)).astype(np.float32)
    meet = np.broadcast_to(meet[:, :, :, None], (slabs, 2, 2 * slabs, 8, cols)).astype(np.float32)
    return sine, sweep, meet, waves, gap


def tiled(plane):
    return plane.reshape(plane.shape[0] // 8, 8, plane.shape[1])


def flat(plane):
    return plane.reshape(plane.shape[0] * 8, plane.shape[2])


def transform(plane, table, extra=None):
    hi = plane.astype(BF16)
    lo = (plane - hi.astype(F32)).astype(BF16)
    parts = [hi, lo] if extra is None else [hi, lo, extra]
    both = jnp.dot(jnp.concatenate(parts, 1), table, preferred_element_type=F32)
    cols = plane.shape[1]
    return both[:, :cols] + both[:, cols : 2 * cols], both[:, 2 * cols :]


def averages(center, above, below):
    cols = center.shape[1]
    lane = lax.broadcasted_iota(jnp.int32, center.shape, 1)
    left = 0.5 * (center + pltpu.roll(center, 1, 1))
    right = 0.5 * (center + pltpu.roll(center, cols - 1, 1))
    up = 0.5 * (center + above)
    down = 0.5 * (center + below)
    zero = jnp.zeros_like(center)
    total = (
        up + down + jnp.where(lane == 0, center, left) + jnp.where(lane == cols - 1, center, right)
    )
    return (
        total,
        jnp.where(lane == 0, zero, left),
        jnp.where(lane == cols - 1, zero, right),
        up,
        down,
    )


def body(
    D,
    NS,
    R,
    list_s,
    count_s,
    guess_h,
    right_h,
    mean_v,
    field_v,
    coup_h,
    fore_v,
    back_v,
    sweep_v,
    meet_v,
    waves_v,
    gap_v,
    sol_h,
    res_h,
    stage_g,
    stage_b,
    stage_r,
    coup_v,
    u,
    sb,
    r0,
    rh,
    strips,
    images,
    outb,
    cin,
    ex,
    low,
    low_ex,
    edge,
    edge_in,
    cpad,
    mco,
    fco,
    lsem,
    hs,
    hr,
    fs,
    fr,
    ps,
    pr,
    os_,
    or_,
    xs,
    xr,
    zs,
    zr,
):
    D2 = D // 2
    N = BLK
    cols = guess_h.shape[1]
    d = lax.axis_index("mode")
    s = lax.axis_index("slab")
    C = d // 2
    p = d % 2
    partner = 2 * C + 1 - p
    above = (s + NS - 1) % NS
    below = (s + 1) % NS
    CH = 32

    def remote(src, dst, send, recv, mode, slab):
        return pltpu.make_async_remote_copy(
            src_ref=src,
            dst_ref=dst,
            send_sem=send,
            recv_sem=recv,
            device_id=(mode, slab),
            device_id_type=pl.DeviceIdType.MESH,
        )

    def landed(ref, sem):
        pltpu.make_async_copy(ref, ref, sem).wait()

    load_g = pltpu.make_async_copy(guess_h, stage_g, lsem.at[0])
    load_b = pltpu.make_async_copy(right_h, stage_b, lsem.at[1])
    load_c = pltpu.make_async_copy(coup_h, coup_v, lsem.at[2])
    load_g.start()
    load_b.start()
    load_c.start()

    barrier = pltpu.get_barrier_semaphore()

    @pl.loop(1, D)
    def _(t):
        pl.semaphore_signal(
            barrier, inc=1, device_id=((d + t) % D, s), device_id_type=pl.DeviceIdType.MESH
        )

    @pl.loop(1, NS)
    def _(t):
        pl.semaphore_signal(
            barrier, inc=1, device_id=(d, (s + t) % NS), device_id_type=pl.DeviceIdType.MESH
        )

    for f in range(FIELDS + 1):
        whole = mean_v[...] if f == 0 else field_v[f - 1]
        cpad[f, pl.ds(8, R), :] = whole
        edge[0, pl.ds(f, 1), :] = whole[:1]
        edge[1, pl.ds(f, 1), :] = whole[R - 1 :]
    images[3 * D] = jnp.zeros((N, 2 * cols), BF16)
    pl.semaphore_wait(barrier, D - 1 + NS - 1)

    coef_up = remote(edge.at[0], edge_in.at[1], hs.at[2], hr.at[2], d, above)
    coef_down = remote(edge.at[1], edge_in.at[0], hs.at[3], hr.at[3], d, below)
    coef_up.start()
    coef_down.start()
    load_g.wait()

    def take(x):
        plane = stage_g[pl.ds(x, N, stride=R), :]
        u[x + 1] = plane
        sb[x + 1] = plane.astype(BF16)

    take(0)
    take(R - 1)
    halo_up = remote(u.at[1], u.at[R + 1], hs.at[0], hr.at[0], d, above)
    halo_down = remote(u.at[R], u.at[0], hs.at[1], hr.at[1], d, below)
    halo_up.start()
    halo_down.start()

    def send_pair(it, i):
        for live, j, half in ((i < D2, 2 * i, 0), (i >= 1, 2 * i - 1, 1)):
            source = sb.at[pl.ds(2 * i, 2)]
            target = strips.at[it, d, pl.ds(2 * half, 2)]

            @pl.when(jnp.logical_and(live, j != d))
            def _():
                remote(source, target, fs.at[it, j], fr.at[it, d], j, s).start()

            @pl.when(jnp.logical_and(live, j == d))
            def _():
                pltpu.make_async_copy(source, target, fr.at[it, d]).start()

    def sent_pairs(it):
        @pl.loop(1, D)
        def _(t):
            j = (d + t) % D
            remote(
                sb.at[pl.ds(0, 2)], strips.at[it, d, pl.ds(0, 2)], fs.at[it, j], fr.at[it, d], j, s
            ).wait_send()

    @pl.loop(0, D2 - 1)
    def _(k):
        i = 1 + (C + k) % (D2 - 1)

        @pl.loop(0, 2)
        def _(h):
            take(2 * i + h - 1)

        send_pair(0, i)

    coef_up.wait()
    coef_down.wait()
    for f in range(FIELDS + 1):
        whole = cpad[f, pl.ds(8, R), :]
        cpad[f, pl.ds(7, 1), :] = jnp.where(s == 0, whole[:1], edge_in[0, pl.ds(f, 1), :])
        cpad[f, pl.ds(8 + R, 1), :] = jnp.where(
            s == NS - 1, whole[R - 1 :], edge_in[1, pl.ds(f, 1), :]
        )
    halo_up.wait()
    halo_down.wait()
    top = jnp.where(s == 0, jnp.zeros((N, cols), F32), u[0])
    bottom = jnp.where(s == NS - 1, jnp.zeros((N, cols), F32), u[R + 1])
    u[0] = top
    u[R + 1] = bottom
    sb[0] = top.astype(BF16)
    sb[R + 1] = bottom.astype(BF16)
    send_pair(0, 0)
    send_pair(0, D2)

    for n, value in enumerate(
        averages(cpad[0, pl.ds(8, R), :], cpad[0, pl.ds(7, R), :], cpad[0, pl.ds(9, R), :])
    ):
        mco[n] = jnp.broadcast_to(value[:, None, :], (R, 8, cols))
    for f in range(FIELDS):
        rows3 = [
            jnp.broadcast_to(cpad[f + 1, pl.ds(7 + d + n, 1), :], (8, cols)) for n in range(3)
        ]
        for n, value in enumerate(averages(rows3[1], rows3[0], rows3[2])):
            fco[f, n] = value
    load_b.wait()
    load_c.wait()

    def apply_mean(x):
        co = [mco[n, x] for n in range(5)]
        for m in range(0, N, CH):
            mid = u[x + 1, pl.ds(m, CH), :]
            left = pltpu.roll(mid, 1, 1)
            right = pltpu.roll(mid, cols - 1, 1)
            total = co[0] * tiled(mid) - co[1] * tiled(left) - co[2] * tiled(right)
            total = total - co[3] * tiled(u[x, pl.ds(m, CH), :])
            total = total - co[4] * tiled(u[x + 2, pl.ds(m, CH), :])
            side = stage_b[pl.ds(m * R + x, CH, stride=R), :]
            r0[x, pl.ds(m, CH), :] = side - flat(total)

    def make_images(it, src):
        for m in range(0, N, CH):
            up, mid, down = (
                strips[it, src, p + n, pl.ds(m, CH), :].astype(F32) for n in range(3)
            )
            left = tiled(pltpu.roll(mid, 1, 1))
            right = tiled(pltpu.roll(mid, cols - 1, 1))
            up, mid, down = tiled(up), tiled(mid), tiled(down)
            for f in range(FIELDS):
                value = flat(
                    fco[f, 0] * mid
                    - fco[f, 1] * left
                    - fco[f, 2] * right
                    - fco[f, 3] * up
                    - fco[f, 4] * down
                )
                hi = value.astype(BF16)
                lo = (value - hi.astype(F32)).astype(BF16)
                images[3 * src + f, pl.ds(m, CH), :cols] = hi
                images[3 * src + f, pl.ds(m, CH), cols:] = lo

    for it in range(ITERS):
        last = it == ITERS - 1

        @pl.loop(0, R)
        def _(x):
            apply_mean(x)

        def source_at(t):
            return 2 * ((C + D2 - t // 2) % D2) + t % 2

        def relay(t):
            src = source_at(t)
            shared = strips.at[it, src, 1 + p]
            return remote(shared, shared, ps.at[it, src], pr.at[it, src], partner, s)

        LAG = 2

        @pl.loop(0, D + LAG)
        def _(t):
            @pl.when(t < D)
            def _():
                src = source_at(t)
                landed(strips.at[it, src, pl.ds(2 * p, 2)], fr.at[it, src])
                relay(t).start()

            @pl.when(t >= LAG)
            def _():
                before = t - LAG
                relay(before).wait_recv()
                make_images(it, source_at(before))

        @pl.loop(0, D)
        def _(t):
            relay(t).wait_send()

        sent_pairs(it)

        def result(i):
            return remote(
                outb.at[it, i], cin.at[it, d], os_.at[it, i], or_.at[it, d], i, s
            )

        @pl.loop(0, D)
        def _(t):
            i = 2 * ((C + 1 + t // 2) % D2) + t % 2
            count = count_s[i]
            lefts = []
            rights = []
            for k in range(MAXC):
                entry = jnp.where(k < count, list_s[i * MAXC + k], 3 * D)
                lefts.append(coup_v[i, k])
                rights.append(images[entry])
            both = jnp.dot(
                jnp.concatenate(lefts, 1),
                jnp.concatenate(rights, 0),
                preferred_element_type=F32,
            )
            outb[it, i] = both[:, :cols] + both[:, cols:]

            @pl.when(i != d)
            def _():
                result(i).start()

            @pl.when(i == d)
            def _():
                pltpu.make_async_copy(outb.at[it, i], cin.at[it, d], or_.at[it, d]).start()

        if not last:
            low[...] = jnp.zeros((N, cols), F32)

        @pl.loop(0, D)
        def _(t):
            x = 2 * ((C + D2 - 1 - t // 2) % D2) + t % 2
            landed(cin.at[it, x], or_.at[it, x])
            plane = r0[x] - cin[it, x]
            if last:
                stage_r[pl.ds(x, N, stride=R), :] = plane
            if last:
                rh[x + 1] = transform(plane, fore_v[:, pl.ds(0, 2 * cols)])[0]
            else:
                rh[x + 1], part = transform(plane, fore_v[...])
                low[...] += flat(tiled(part) * waves_v[s, x + 1])

        @pl.loop(1, D)
        def _(t):
            result((d + t) % D).wait_send()

        if last:
            store_r = pltpu.make_async_copy(stage_r, res_h, lsem.at[3])
            store_r.start()

        @pl.loop(0, N // CH)
        def _(c):
            m = pl.multiple_of(c * CH, CH)
            ms = pl.ds(m, CH)
            run = jnp.zeros((CH // 8, 8, cols), F32)
            head = jnp.zeros((CH // 8, 8, cols), F32)
            for x in range(R):
                value = tiled(rh[x + 1, ms, :])
                head = head + sweep_v[1, x] * value
                run = (run + value) * sweep_v[0, x]
                rh[x + 1, ms, :] = flat(run)
            ex[it, s, 0, ms, :] = flat(head)
            ex[it, s, 1, ms, :] = flat(run)

        def swap(t):
            mine = ex.at[it, s]
            return remote(mine, mine, xs.at[it, t], xr.at[it, s], d, (s + t) % NS)

        def swap_low(t):
            mine = low_ex.at[s]
            return remote(mine, mine, zs.at[t], zr.at[s], d, (s + t) % NS)

        if not last:
            low_ex[s] = low[...].astype(BF16)

        @pl.loop(1, NS)
        def _(t):
            swap(t).start()
            if not last:
                swap_low(t).start()

        @pl.loop(1, NS)
        def _(t):
            other = (s + t) % NS
            landed(ex.at[it, other], xr.at[it, other])
            if not last:
                landed(low_ex.at[other], zr.at[other])

        @pl.loop(0, N // CH)
        def _(c):
            m = pl.multiple_of(c * CH, CH)
            ms = pl.ds(m, CH)
            ends = [tiled(ex[it, k % NS, k // NS, ms, :]) for k in range(2 * NS)]
            outer = []
            for side in range(2):
                total = meet_v[s, side, 0] * ends[0]
                for k in range(1, 2 * NS):
                    total = total + meet_v[s, side, k] * ends[k]
                outer.append(total)
            rh[0, ms, :] = flat(outer[0])
            rh[R + 1, ms, :] = flat(outer[1])
            run = outer[1]
            for x in reversed(range(R)):
                run = tiled(rh[x + 1, ms, :]) + sweep_v[2, x] * outer[0] + sweep_v[0, x] * run
                rh[x + 1, ms, :] = flat(run)

        @pl.loop(1, NS)
        def _(t):
            swap(t).wait_send()
            if not last:
                swap_low(t).wait_send()

        if last:

            @pl.loop(0, R)
            def _(x):
                plane = u[x + 1] + transform(rh[x + 1], back_v[pl.ds(0, 2 * cols), :])[0]
                stage_g[pl.ds(x, N, stride=R), :] = plane

        else:
            total = low_ex[0].astype(F32)
            for k in range(1, NS):
                total = total + low_ex[k].astype(F32)
            low[...] = flat(tiled(total) * gap_v[...])

            @pl.loop(0, D2 + 1)
            def _(k):
                i = (C + k) % (D2 + 1)

                @pl.loop(0, 2)
                def _(h):
                    x = 2 * i + h
                    wave = flat(tiled(low[...]) * waves_v[s, x]).astype(BF16)
                    plane = u[x] + transform(rh[x], back_v[...], wave)[0]
                    u[x] = plane
                    sb[x] = plane.astype(BF16)

                send_pair(it + 1, i)

    store_s = pltpu.make_async_copy(stage_g, sol_h, lsem.at[4])
    store_s.start()
    store_r.wait()
    store_s.wait()


def local(D, NS, interpret, guess, right_side, mean_coef, field_coef, coupling, listed, count):
    modes, R, cols = guess.shape
    N = BLK
    sine, sweep, meet, waves, gap = tables(R, cols, NS)
    fore = fore_table(sine)
    back = back_table(RELAX * sine.astype(np.float64))
    flat_shape = jax.ShapeDtypeStruct((modes * R, cols), F32)
    hbm = pl.BlockSpec(memory_space=pl.ANY)
    vmem = pl.BlockSpec(memory_space=pltpu.VMEM)
    smem = pl.BlockSpec(memory_space=pltpu.SMEM)
    sems = pltpu.SemaphoreType.DMA
    sol, res = pl.pallas_call(
        functools.partial(body, D, NS, R),
        out_shape=(flat_shape, flat_shape),
        in_specs=[smem, smem, hbm, hbm, vmem, vmem, hbm] + [vmem] * 6,
        out_specs=(hbm, hbm),
        scratch_shapes=[
            pltpu.VMEM((modes * R, cols), F32),
            pltpu.VMEM((modes * R, cols), F32),
            pltpu.VMEM((modes * R, cols), F32),
            pltpu.VMEM((D, MAXC, N, N), BF16),
            pltpu.VMEM((R + 2, N, cols), F32),
            pltpu.VMEM((R + 2, N, cols), BF16),
            pltpu.VMEM((R, N, cols), F32),
            pltpu.VMEM((R + 2, N, cols), F32),
            pltpu.VMEM((ITERS, D, 4, N, cols), BF16),
            pltpu.VMEM((FIELDS * D + 1, N, 2 * cols), BF16),
            pltpu.VMEM((ITERS, D, N, cols), F32),
            pltpu.VMEM((ITERS, R, N, cols), F32),
            pltpu.VMEM((ITERS, NS, 2, N, cols), F32),
            pltpu.VMEM((N, cols), F32),
            pltpu.VMEM((NS, N, cols), BF16),
            pltpu.VMEM((2, 8, cols), F32),
            pltpu.VMEM((2, 8, cols), F32),
            pltpu.VMEM((FIELDS + 1, R + 16, cols), F32),
            pltpu.VMEM((5, R, 8, cols), F32),
            pltpu.VMEM((FIELDS, 5, 8, cols), F32),
            sems((5,)),
            sems((4,)),
            sems((4,)),
            sems((ITERS, D)),
            sems((ITERS, D)),
            sems((ITERS, D)),
            sems((ITERS, D)),
            sems((ITERS, D)),
            sems((ITERS, D)),
            sems((ITERS, NS)),
            sems((ITERS, NS)),
            sems((NS,)),
            sems((NS,)),
        ],
        compiler_params=pltpu.CompilerParams(
            collective_id=0, has_side_effects=True, vmem_limit_bytes=67043328
        ),
        interpret=interpret,
    )(
        listed.reshape(-1),
        count,
        guess.reshape(modes * R, cols),
        right_side.reshape(modes * R, cols),
        mean_coef,
        field_coef,
        coupling,
        *(jnp.asarray(table) for table in (fore, back, sweep, meet, waves, gap)),
    )
    return sol.reshape(guess.shape), res.reshape(guess.shape)


def solution(mesh, interpret=False):
    placed = (
        P("mode", "slab", None),
        P("mode", "slab", None),
        P("slab", None),
        P(None, "slab", None),
        P(),
        P(),
        P(),
    )
    return jax.shard_map(
        functools.partial(local, mesh.shape["mode"], mesh.shape["slab"], interpret),
        mesh=mesh,
        in_specs=placed,
        out_specs=(P("mode", "slab", None), P("mode", "slab", None)),
        check_vma=False,
    )
```

time: 600 us -> 192 us (0.32); the launches traced: 589 us -> 192 us
  blocking collectives: 288 us -> 0 us
  Pallas kernels: 0 us -> 185 us
  waiting for transfers between devices: 88.6 us -> 0 us
  matrix products: 82.8 us -> 0 us
  local copies, waits for them, and re-layouts: 67.9 us -> 5.98 us
  other arithmetic: 31.9 us -> 0 us
  starting transfers between devices: 27.7 us -> 0 us
    all_to_all x9 -> x0, blocking collectives: 288 us -> none  [the longest x6 205 us: cut_exchange(): lax.all_to_all(slab, axis, split_axis=0, concat_axis=0, tiled=True)]
    pallas_call x0 -> x1, Pallas kernels: none -> 185 us  [local(): pl.pallas_call(functools.partial(body, D, NS, R), out_shape=(flat_shape,...]
    dot_general x10 -> x0, matrix products: 82.8 us -> none  [the longest x2 52.5 us: local(): jnp.einsum('ikab,ikbc->iac', coupling.astype(jnp.float32), gathered, prec...]
    all_to_all x3 -> x0, waiting for transfers between devices: 81.7 us -> none  [the longest x2 56.1 us: cut_exchange(): lax.all_to_all(slab, axis, split_axis=0, concat_axis=0, tiled=True)]
    gather x2 -> x0, local copies, waits for them, and re-layouts: 37.2 us -> none  [local(): strip_images[field_index, partner]]
    ppermute x6 -> x0, starting transfers between devices: 14 us -> none  [the longest x3 10.1 us: with_halo(): lax.ppermute(lax.slice_in_dim(block, block.shape[dim] - width, None, axis...]
    all_to_all x3 -> x0, starting transfers between devices: 13.7 us -> none  [the longest x2 9.58 us: cut_exchange(): lax.all_to_all(slab, axis, split_axis=0, concat_axis=0, tiled=True)]
    transpose x2 -> x0, other arithmetic: 8.16 us -> none  [laid_out(): return jnp.moveaxis(blocks, 0, dim).reshape(lengths)]
  transfers between devices with their start and end apart: 9 -> 0, of which waited for: 5 -> 0; matrix products, arithmetic and copies ran while one was open for 1% -> 0% of each run, Pallas kernels for 0% -> 0%
where the time goes in v1:
time: 192 us
  Pallas kernels  185 us (96%)
  local copies, waits for them, and re-layouts  5.98 us (3%)
    pallas_call x1, Pallas kernels, local(): pl.pallas_call(functools.partial(body, D, NS, R), out_shape=(flat_shape,...  185 us
    unnamed x5, local copies, waits for them, and re-layouts  5.32 us

profile of v1, /device:TPU:1, one launch (start us, length us, event | category | flops | bytes accessed | tf_op | source)
XLA Modules:
  0.0 191.9 jit_solution(8368519940528751330)
XLA Ops:
  0.6 0.8 copy.15
  1.4 0.7 reshape.19.list_s
  2.1 185.3 %shard_map.140 = (f32[4096,128]{1,0:T(8,128)}, f32[4096,128]{1,0:T(8,128)}) custom-call(s32[512]{0:T(512)} %reshape.19.list_s, s32[32]{0:T(128)} %count_s.1, f32[4096,128]{1,0:T(8,128)} %bitcast.4, f32[4096,128]{1,0:T(8,128)} %bitcast.5, f32[32,128]{1,0:T(8,128)} %mean_v.1, f32[3,32,128]{2,1,0:T(8,128)} %field_v.1, bf16[32,16,128,128]{3,2,1,0:T(8,128)(2,1)} %coup_h.1, ...), custom_call_target="tpu_custom_call" | custom-call | tf_op jit(solution)/shard_map/pallas_call | solution.py:566
  187.3 0.0 copy-start
  187.3 3.2 %copy.18 = f32[128,32,128]{2,1,0:T(8,128)} copy(f32[128,32,128]{2,1,0:T(8,128)} %bitcast.7) | data formatting | bytes 4194304
  190.6 0.0 copy-done
  190.6 1.3 copy.19
Async XLA Ops:
  187.3 3.2 %copy-start = (f32[4096,128]{1,0:T(8,128)S(1)}, f32[4096,128]{1,0:T(8,128)}, u32[]{:S(2)}) copy-start(f32[4096,128]{1,0:T(8,128)} %get-tuple-element.5) | copy-start | bytes 6291460

commit v2 on v1

--- a/solution.py
+++ b/solution.py
@@ -14,6 +14,7 @@
 BLK = 128
 ITERS = 2
 RELAX = 0.6
+STEPS = 32760.0
 F32 = jnp.float32
 BF16 = jnp.bfloat16
 
@@ -156,17 +157,21 @@
     mean_v,
     field_v,
     coup_h,
+    fore_h,
+    back_h,
+    sweep_h,
+    meet_h,
+    waves_h,
+    gap_v,
+    sol_h,
+    res_h,
+    stage_g,
+    stage_b,
     fore_v,
     back_v,
     sweep_v,
     meet_v,
     waves_v,
-    gap_v,
-    sol_h,
-    res_h,
-    stage_g,
-    stage_b,
-    stage_r,
     coup_v,
     u,
     sb,
@@ -174,8 +179,10 @@
     rh,
     strips,
     images,
-    outb,
-    cin,
+    outq,
+    outs,
+    inq,
+    ins,
     ex,
     low,
     low_ex,
@@ -197,10 +204,13 @@
     xr,
     zs,
     zr,
+    table_sem,
+    coup_sem,
 ):
     D2 = D // 2
     N = BLK
     cols = guess_h.shape[1]
+    WINDOW = min(4, D2 - 1)
     d = lax.axis_index("mode")
     s = lax.axis_index("slab")
     C = d // 2
@@ -223,12 +233,27 @@
     def landed(ref, sem):
         pltpu.make_async_copy(ref, ref, sem).wait()
 
+    HM = N // 2
     load_g = pltpu.make_async_copy(guess_h, stage_g, lsem.at[0])
     load_b = pltpu.make_async_copy(right_h, stage_b, lsem.at[1])
-    load_c = pltpu.make_async_copy(coup_h, coup_v, lsem.at[2])
     load_g.start()
-    load_b.start()
-    load_c.start()
+
+    def load_coupling(k):
+        some = pl.ds(2 * k, 2)
+        return pltpu.make_async_copy(coup_h.at[some], coup_v.at[some], coup_sem.at[k])
+
+    table_loads = [
+        pltpu.make_async_copy(source, target, table_sem.at[n])
+        for n, (source, target) in enumerate(
+            (
+                (fore_h, fore_v),
+                (back_h, back_v),
+                (sweep_h, sweep_v),
+                (meet_h.at[s], meet_v),
+                (waves_h.at[s], waves_v),
+            )
+        )
+    ]
 
     barrier = pltpu.get_barrier_semaphore()
 
@@ -250,12 +275,6 @@
         edge[0, pl.ds(f, 1), :] = whole[:1]
         edge[1, pl.ds(f, 1), :] = whole[R - 1 :]
     images[3 * D] = jnp.zeros((N, 2 * cols), BF16)
-    pl.semaphore_wait(barrier, D - 1 + NS - 1)
-
-    coef_up = remote(edge.at[0], edge_in.at[1], hs.at[2], hr.at[2], d, above)
-    coef_down = remote(edge.at[1], edge_in.at[0], hs.at[3], hr.at[3], d, below)
-    coef_up.start()
-    coef_down.start()
     load_g.wait()
 
     def take(x):
@@ -265,41 +284,71 @@
 
     take(0)
     take(R - 1)
+    pl.semaphore_wait(barrier, D - 1 + NS - 1)
+
     halo_up = remote(u.at[1], u.at[R + 1], hs.at[0], hr.at[0], d, above)
     halo_down = remote(u.at[R], u.at[0], hs.at[1], hr.at[1], d, below)
+    coef_up = remote(edge.at[0], edge_in.at[1], hs.at[2], hr.at[2], d, above)
+    coef_down = remote(edge.at[1], edge_in.at[0], hs.at[3], hr.at[3], d, below)
     halo_up.start()
     halo_down.start()
-
-    def send_pair(it, i):
+    coef_up.start()
+    coef_down.start()
+
+    def pair_copies(it, i, g):
+        source = sb.at[pl.ds(2 * i, 2), pl.ds(g * HM, HM)]
         for live, j, half in ((i < D2, 2 * i, 0), (i >= 1, 2 * i - 1, 1)):
-            source = sb.at[pl.ds(2 * i, 2)]
-            target = strips.at[it, d, pl.ds(2 * half, 2)]
+            target = strips.at[it, d, pl.ds(2 * half, 2), pl.ds(g * HM, HM)]
+            yield live, j, source, target
+
+    def send_pair(it, i, g):
+        for live, j, source, target in pair_copies(it, i, g):
 
             @pl.when(jnp.logical_and(live, j != d))
             def _():
-                remote(source, target, fs.at[it, j], fr.at[it, d], j, s).start()
+                remote(source, target, fs.at[it, g, j], fr.at[it, g, d], j, s).start()
 
             @pl.when(jnp.logical_and(live, j == d))
             def _():
-                pltpu.make_async_copy(source, target, fr.at[it, d]).start()
+                pltpu.make_async_copy(source, target, fr.at[it, g, d]).start()
 
     def sent_pairs(it):
         @pl.loop(1, D)
         def _(t):
             j = (d + t) % D
-            remote(
-                sb.at[pl.ds(0, 2)], strips.at[it, d, pl.ds(0, 2)], fs.at[it, j], fr.at[it, d], j, s
-            ).wait_send()
-
-    @pl.loop(0, D2 - 1)
+            for g in range(2):
+                source = sb.at[pl.ds(0, 2), pl.ds(g * HM, HM)]
+                target = strips.at[it, d, pl.ds(0, 2), pl.ds(g * HM, HM)]
+                remote(source, target, fs.at[it, g, j], fr.at[it, g, d], j, s).wait_send()
+
+    def pair_at(it, k):
+        return 1 + (C + D2 - 2 + k) % (D2 - 1) if it == 0 else (C + k) % (D2 + 1)
+
+    def pairs(it):
+        return D2 - 1 if it == 0 else D2 + 1
+
+    def take_pair(k):
+        i = pair_at(0, k)
+        for h in range(2):
+            x = 2 * i + h - 1
+
+            @pl.when(jnp.logical_and(x != 0, x != R - 1))
+            def _():
+                take(x)
+
+    @pl.loop(0, WINDOW)
     def _(k):
-        i = 1 + (C + k) % (D2 - 1)
-
-        @pl.loop(0, 2)
-        def _(h):
-            take(2 * i + h - 1)
-
-        send_pair(0, i)
+        take_pair(k)
+        for g in range(2):
+            send_pair(0, pair_at(0, k), g)
+
+    load_b.start()
+    for copy in table_loads:
+        copy.start()
+
+    @pl.loop(WINDOW, D2 - 1)
+    def _(k):
+        take_pair(k)
 
     coef_up.wait()
     coef_down.wait()
@@ -317,8 +366,9 @@
     u[R + 1] = bottom
     sb[0] = top.astype(BF16)
     sb[R + 1] = bottom.astype(BF16)
-    send_pair(0, 0)
-    send_pair(0, D2)
+    for g in range(2):
+        send_pair(0, 0, g)
+        send_pair(0, D2, g)
 
     for n, value in enumerate(
         averages(cpad[0, pl.ds(8, R), :], cpad[0, pl.ds(7, R), :], cpad[0, pl.ds(9, R), :])
@@ -331,7 +381,8 @@
         for n, value in enumerate(averages(rows3[1], rows3[0], rows3[2])):
             fco[f, n] = value
     load_b.wait()
-    load_c.wait()
+    for copy in table_loads:
+        copy.wait()
 
     def apply_mean(x):
         co = [mco[n, x] for n in range(5)]
@@ -369,53 +420,78 @@
     for it in range(ITERS):
         last = it == ITERS - 1
 
-        @pl.loop(0, R)
-        def _(x):
-            apply_mean(x)
-
-        def source_at(t):
-            return 2 * ((C + D2 - t // 2) % D2) + t % 2
-
-        def relay(t):
-            src = source_at(t)
+        def source_at(k, q):
+            return 2 * ((C + D2 - k) % D2) + q
+
+        def relay(k, q):
+            src = source_at(k, q)
             shared = strips.at[it, src, 1 + p]
             return remote(shared, shared, ps.at[it, src], pr.at[it, src], partner, s)
 
-        LAG = 2
-
-        @pl.loop(0, D + LAG)
-        def _(t):
-            @pl.when(t < D)
+        def arrive(k):
+            for q in range(2):
+                src = source_at(k, q)
+                for g in range(2):
+                    landed(
+                        strips.at[it, src, pl.ds(2 * p, 2), pl.ds(g * HM, HM)], fr.at[it, g, src]
+                    )
+                relay(k, q).start()
+
+        def imagine(k):
+            for q in range(2):
+                relay(k, q).wait_recv()
+            for q in range(2):
+                make_images(it, source_at(k, q))
+
+        def send_next(k):
+            @pl.when(k + WINDOW < pairs(it))
             def _():
-                src = source_at(t)
-                landed(strips.at[it, src, pl.ds(2 * p, 2)], fr.at[it, src])
-                relay(t).start()
-
-            @pl.when(t >= LAG)
-            def _():
-                before = t - LAG
-                relay(before).wait_recv()
-                make_images(it, source_at(before))
-
-        @pl.loop(0, D)
-        def _(t):
-            relay(t).wait_send()
+                for g in range(2):
+                    send_pair(it, pair_at(it, k + WINDOW), g)
+
+            if it == 0:
+                load_coupling(k).start()
+
+        arrive(0)
+        send_next(0)
+        apply_mean(0)
+        apply_mean(1)
+
+        @pl.loop(1, D2)
+        def _(k):
+            arrive(k)
+            send_next(k)
+            imagine(k - 1)
+            apply_mean(2 * k)
+            apply_mean(2 * k + 1)
+
+        imagine(D2 - 1)
+
+        @pl.loop(0, D2)
+        def _(k):
+            for q in range(2):
+                relay(k, q).wait_send()
 
         sent_pairs(it)
-
-        def result(i):
-            return remote(
-                outb.at[it, i], cin.at[it, d], os_.at[it, i], or_.at[it, d], i, s
+        if it == 0:
+
+            @pl.loop(0, D2)
+            def _(k):
+                load_coupling(k).wait()
+
+
+        def results(i):
+            return (
+                remote(outq.at[it, i], inq.at[it, d], os_.at[it, 0, i], or_.at[it, 0, d], i, s),
+                remote(outs.at[it, i], ins.at[it, d], os_.at[it, 1, i], or_.at[it, 1, d], i, s),
             )
 
-        @pl.loop(0, D)
-        def _(t):
-            i = 2 * ((C + 1 + t // 2) % D2) + t % 2
+        def mix(i):
             count = count_s[i]
             lefts = []
             rights = []
             for k in range(MAXC):
-                entry = jnp.where(k < count, list_s[i * MAXC + k], 3 * D)
+                entry = jnp.where(k < count, list_s[k, i], 3 * D)
                 lefts.append(coup_v[i, k])
                 rights.append(images[entry])
             both = jnp.dot(
@@ -423,57 +499,58 @@
                 jnp.concatenate(rights, 0),
                 preferred_element_type=F32,
             )
-            outb[it, i] = both[:, :cols] + both[:, cols:]
-
-            @pl.when(i != d)
-            def _():
-                result(i).start()
-
-            @pl.when(i == d)
-            def _():
-                pltpu.make_async_copy(outb.at[it, i], cin.at[it, d], or_.at[it, d]).start()
+            value = both[:, :cols] + both[:, cols:]
+            peak = jnp.max(jnp.abs(value), axis=0, keepdims=True)
+            peak = jnp.maximum(peak, 1e-30)
+            outq[it, i] = jnp.round(value * (STEPS / peak)).astype(jnp.int16)
+            outs[it, i] = peak * (1.0 / STEPS)
+
+        @pl.loop(1, D2)
+        def _(k):
+            i = 2 * ((C + k) % D2)
+            mix(i)
+            mix(i + 1)
+            for q in range(2):
+                for copy in results(i + q):
+                    copy.start()
+
+        mix(2 * C)
+        mix(2 * C + 1)
+        for copy in results(partner):
+            copy.start()
+        pltpu.make_async_copy(outq.at[it, d], inq.at[it, d], or_.at[it, 0, d]).start()
+        pltpu.make_async_copy(outs.at[it, d], ins.at[it, d], or_.at[it, 1, d]).start()
 
         if not last:
             low[...] = jnp.zeros((N, cols), F32)
 
-        @pl.loop(0, D)
-        def _(t):
-            x = 2 * ((C + D2 - 1 - t // 2) % D2) + t % 2
-            landed(cin.at[it, x], or_.at[it, x])
-            plane = r0[x] - cin[it, x]
-            if last:
-                stage_r[pl.ds(x, N, stride=R), :] = plane
-            if last:
-                rh[x + 1] = transform(plane, fore_v[:, pl.ds(0, 2 * cols)])[0]
-            else:
-                rh[x + 1], part = transform(plane, fore_v[...])
-                low[...] += flat(tiled(part) * waves_v[s, x + 1])
+        @pl.loop(0, D2)
+        def _(k):
+            a = 2 * ((C + 2 * D2 - 1 - k) % D2)
+            for q in range(2):
+                landed(inq.at[it, a + q], or_.at[it, 0, a + q])
+                landed(ins.at[it, a + q], or_.at[it, 1, a + q])
+            parts = []
+            for q in range(2):
+                x = a + q
+                plane = r0[x] - inq[it, x].astype(F32) * ins[it, x]
+                if last:
+                    stage_b[pl.ds(x, N, stride=R), :] = plane
+                    rh[x + 1] = transform(plane, fore_v[:, pl.ds(0, 2 * cols)])[0]
+                else:
+                    rh[x + 1], part = transform(plane, fore_v[...])
+                    parts.append(tiled(part) * waves_v[x + 1])
+            if not last:
+                low[...] += flat(parts[0] + parts[1])
 
         @pl.loop(1, D)
         def _(t):
-            result((d + t) % D).wait_send()
+            for copy in results((d + t) % D):
+                copy.wait_send()
 
         if last:
-            store_r = pltpu.make_async_copy(stage_r, res_h, lsem.at[3])
+            store_r = pltpu.make_async_copy(stage_b, res_h, lsem.at[2])
             store_r.start()
-
-        @pl.loop(0, N // CH)
-        def _(c):
-            m = pl.multiple_of(c * CH, CH)
-            ms = pl.ds(m, CH)
-            run = jnp.zeros((CH // 8, 8, cols), F32)
-            head = jnp.zeros((CH // 8, 8, cols), F32)
-            for x in range(R):
-                value = tiled(rh[x + 1, ms, :])
-                head = head + sweep_v[1, x] * value
-                run = (run + value) * sweep_v[0, x]
-                rh[x + 1, ms, :] = flat(run)
-            ex[it, s, 0, ms, :] = flat(head)
-            ex[it, s, 1, ms, :] = flat(run)
-
-        def swap(t):
-            mine = ex.at[it, s]
-            return remote(mine, mine, xs.at[it, t], xr.at[it, s], d, (s + t) % NS)
 
         def swap_low(t):
             mine = low_ex.at[s]
@@ -482,74 +559,113 @@
         if not last:
             low_ex[s] = low[...].astype(BF16)
 
+            @pl.loop(1, NS)
+            def _(t):
+                swap_low(t).start()
+
+        def swap(t, g):
+            mine = ex.at[it, g, s]
+            return remote(mine, mine, xs.at[it, g, t], xr.at[it, g, s], d, (s + t) % NS)
+
+        for g in range(2):
+
+            @pl.loop(0, HM // CH)
+            def _(c):
+                m = pl.multiple_of(c * CH, CH)
+                ms = pl.ds(g * HM + m, CH)
+                run = jnp.zeros((CH // 8, 8, cols), F32)
+                head = jnp.zeros((CH // 8, 8, cols), F32)
+                for x in range(R):
+                    value = tiled(rh[x + 1, ms, :])
+                    head = head + sweep_v[1, x] * value
+                    run = (run + value) * sweep_v[0, x]
+                    rh[x + 1, ms, :] = flat(run)
+                ex[it, g, s, 0, pl.ds(m, CH), :] = flat(head)
+                ex[it, g, s, 1, pl.ds(m, CH), :] = flat(run)
+
+            @pl.loop(1, NS)
+            def _(t):
+                swap(t, g).start()
+
+        for g in range(2):
+
+            @pl.loop(1, NS)
+            def _(t):
+                other = (s + t) % NS
+                landed(ex.at[it, g, other], xr.at[it, g, other])
+
+            @pl.loop(0, HM // CH)
+            def _(c):
+                m = pl.multiple_of(c * CH, CH)
+                ms = pl.ds(g * HM + m, CH)
+                ends = [tiled(ex[it, g, k % NS, k // NS, pl.ds(m, CH), :]) for k in range(2 * NS)]
+                outer = []
+                for side_of in range(2):
+                    total = meet_v[side_of, 0] * ends[0]
+                    for k in range(1, 2 * NS):
+                        total = total + meet_v[side_of, k] * ends[k]
+                    outer.append(total)
+                rh[0, ms, :] = flat(outer[0])
+                rh[R + 1, ms, :] = flat(outer[1])
+                run = outer[1]
+                for x in reversed(range(R)):
+                    run = (
+                        tiled(rh[x + 1, ms, :]) + sweep_v[2, x] * outer[0] + sweep_v[0, x] * run
+                    )
+                    rh[x + 1, ms, :] = flat(run)
+
+            half = pl.ds(g * HM, HM)
+            if last:
+
+                @pl.loop(0, D2)
+                def _(i):
+                    for h in range(2):
+                        x = 2 * i + h + 1
+                        change = transform(rh[x, half, :], back_v[pl.ds(0, 2 * cols), :])[0]
+                        whole = pl.ds(g * HM * R + x - 1, HM, stride=R)
+                        stage_g[whole, :] = u[x, half, :] + change
+
+                part = pl.ds(g * HM * R, HM * R)
+                pltpu.make_async_copy(stage_g.at[part], sol_h.at[part], lsem.at[3 + g]).start()
+
+            else:
+                if g == 0:
+
+                    @pl.loop(1, NS)
+                    def _(t):
+                        other = (s + t) % NS
+                        landed(low_ex.at[other], zr.at[other])
+
+                    total = low_ex[0].astype(F32)
+                    for k in range(1, NS):
+                        total = total + low_ex[k].astype(F32)
+                    low[...] = flat(tiled(total) * gap_v[...])
+
+                @pl.loop(0, D2 + 1)
+                def _(k):
+                    i = (C + k) % (D2 + 1)
+                    for h in range(2):
+                        x = 2 * i + h
+                        wave = flat(tiled(low[half, :]) * waves_v[x]).astype(BF16)
+                        plane = u[x, half, :] + transform(rh[x, half, :], back_v[...], wave)[0]
+                        u[x, half, :] = plane
+                        sb[x, half, :] = plane.astype(BF16)
+
+                    @pl.when(k < WINDOW)
+                    def _():
+                        send_pair(it + 1, i, g)
+
         @pl.loop(1, NS)
         def _(t):
-            swap(t).start()
-            if not last:
-                swap_low(t).start()
-
-        @pl.loop(1, NS)
-        def _(t):
-            other = (s + t) % NS
-            landed(ex.at[it, other], xr.at[it, other])
-            if not last:
-                landed(low_ex.at[other], zr.at[other])
-
-        @pl.loop(0, N // CH)
-        def _(c):
-            m = pl.multiple_of(c * CH, CH)
-            ms = pl.ds(m, CH)
-            ends = [tiled(ex[it, k % NS, k // NS, ms, :]) for k in range(2 * NS)]
-            outer = []
-            for side in range(2):
-                total = meet_v[s, side, 0] * ends[0]
-                for k in range(1, 2 * NS):
-                    total = total + meet_v[s, side, k] * ends[k]
-                outer.append(total)
-            rh[0, ms, :] = flat(outer[0])
-            rh[R + 1, ms, :] = flat(outer[1])
-            run = outer[1]
-            for x in reversed(range(R)):
-                run = tiled(rh[x + 1, ms, :]) + sweep_v[2, x] * outer[0] + sweep_v[0, x] * run
-                rh[x + 1, ms, :] = flat(run)
-
-        @pl.loop(1, NS)
-        def _(t):
-            swap(t).wait_send()
+            for g in range(2):
+                swap(t, g).wait_send()
             if not last:
                 swap_low(t).wait_send()
 
-        if last:
-
-            @pl.loop(0, R)
-            def _(x):
-                plane = u[x + 1] + transform(rh[x + 1], back_v[pl.ds(0, 2 * cols), :])[0]
-                stage_g[pl.ds(x, N, stride=R), :] = plane
-
-        else:
-            total = low_ex[0].astype(F32)
-            for k in range(1, NS):
-                total = total + low_ex[k].astype(F32)
-            low[...] = flat(tiled(total) * gap_v[...])
-
-            @pl.loop(0, D2 + 1)
-            def _(k):
-                i = (C + k) % (D2 + 1)
-
-                @pl.loop(0, 2)
-                def _(h):
-                    x = 2 * i + h
-                    wave = flat(tiled(low[...]) * waves_v[s, x]).astype(BF16)
-                    plane = u[x] + transform(rh[x], back_v[...], wave)[0]
-                    u[x] = plane
-                    sb[x] = plane.astype(BF16)
-
-                send_pair(it + 1, i)
-
-    store_s = pltpu.make_async_copy(stage_g, sol_h, lsem.at[4])
-    store_s.start()
     store_r.wait()
-    store_s.wait()
+    for g in range(2):
+        part = pl.ds(g * HM * R, HM * R)
+        pltpu.make_async_copy(stage_g.at[part], sol_h.at[part], lsem.at[3 + g]).wait()
 
 
 def local(D, NS, interpret, guess, right_side, mean_coef, field_coef, coupling, listed, count):
@@ -566,12 +682,16 @@
     sol, res = pl.pallas_call(
         functools.partial(body, D, NS, R),
         out_shape=(flat_shape, flat_shape),
-        in_specs=[smem, smem, hbm, hbm, vmem, vmem, hbm] + [vmem] * 6,
+        in_specs=[smem, smem, hbm, hbm, vmem, vmem, hbm] + [hbm] * 5 + [vmem],
         out_specs=(hbm, hbm),
         scratch_shapes=[
             pltpu.VMEM((modes * R, cols), F32),
             pltpu.VMEM((modes * R, cols), F32),
-            pltpu.VMEM((modes * R, cols), F32),
+            pltpu.VMEM(fore.shape, BF16),
+            pltpu.VMEM(back.shape, BF16),
+            pltpu.VMEM(sweep.shape, F32),
+            pltpu.VMEM(meet.shape[1:], F32),
+            pltpu.VMEM(waves.shape[1:], F32),
             pltpu.VMEM((D, MAXC, N, N), BF16),
             pltpu.VMEM((R + 2, N, cols), F32),
             pltpu.VMEM((R + 2, N, cols), BF16),
@@ -579,9 +699,11 @@
             pltpu.VMEM((R + 2, N, cols), F32),
             pltpu.VMEM((ITERS, D, 4, N, cols), BF16),
             pltpu.VMEM((FIELDS * D + 1, N, 2 * cols), BF16),
-            pltpu.VMEM((ITERS, D, N, cols), F32),
-            pltpu.VMEM((ITERS, R, N, cols), F32),
-            pltpu.VMEM((ITERS, NS, 2, N, cols), F32),
+            pltpu.VMEM((ITERS, D, N, cols), jnp.int16),
+            pltpu.VMEM((ITERS, D, 1, cols), F32),
+            pltpu.VMEM((ITERS, R, N, cols), jnp.int16),
+            pltpu.VMEM((ITERS, R, 1, cols), F32),
+            pltpu.VMEM((ITERS, 2, NS, 2, N // 2, cols), F32),
             pltpu.VMEM((N, cols), F32),
             pltpu.VMEM((NS, N, cols), BF16),
             pltpu.VMEM((2, 8, cols), F32),
@@ -592,23 +714,25 @@
             sems((5,)),
             sems((4,)),
             sems((4,)),
+            sems((ITERS, 2, D)),
+            sems((ITERS, 2, D)),
             sems((ITERS, D)),
             sems((ITERS, D)),
-            sems((ITERS, D)),
-            sems((ITERS, D)),
-            sems((ITERS, D)),
-            sems((ITERS, D)),
-            sems((ITERS, NS)),
-            sems((ITERS, NS)),
+            sems((ITERS, 2, D)),
+            sems((ITERS, 2, D)),
+            sems((ITERS, 2, NS)),
+            sems((ITERS, 2, NS)),
             sems((NS,)),
             sems((NS,)),
+            sems((5,)),
+            sems((D // 2,)),
         ],
         compiler_params=pltpu.CompilerParams(
             collective_id=0, has_side_effects=True, vmem_limit_bytes=67043328
         ),
         interpret=interpret,
     )(
-        listed.reshape(-1),
+        listed.T,
         count,
         guess.reshape(modes * R, cols),
         right_side.reshape(modes * R, cols),

time: 192 us -> 178 us (0.927)
  Pallas kernels: 185 us -> 172 us
    pallas_call x1, Pallas kernels: 185 us -> 172 us  [local(): pl.pallas_call(functools.partial(body, D, NS, R), out_shape=(flat_shape,...]
    unnamed x5 -> x4, local copies, waits for them, and re-layouts: 5.32 us -> 4.55 us
where the time goes in v2:
time: 178 us; the launch traced here: 177 us
  Pallas kernels  172 us (97%)
  local copies, waits for them, and re-layouts  4.55 us (3%)
    pallas_call x1, Pallas kernels, local(): pl.pallas_call(functools.partial(body, D, NS, R), out_shape=(flat_shape,...  172 us
    unnamed x4, local copies, waits for them, and re-layouts  4.55 us

profile of v2, /device:TPU:1, one launch (start us, length us, event | category | flops | bytes accessed | tf_op | source)
XLA Modules:
  0.0 177.3 jit_solution(16330513851634842756)
XLA Ops:
  0.6 172.1 %shard_map.140 = (f32[4096,128]{1,0:T(8,128)}, f32[4096,128]{1,0:T(8,128)}) custom-call(s32[16,32]{1,0:T(8,128)} %bitcast.9, s32[32]{0:T(128)} %count_s.1, f32[4096,128]{1,0:T(8,128)} %bitcast.5, f32[4096,128]{1,0:T(8,128)} %bitcast.6, f32[32,128]{1,0:T(8,128)} %mean_v.1, f32[3,32,128]{2,1,0:T(8,128)} %field_v.1, bf16[32,16,128,128]{3,2,1,0:T(8,128)(2,1)} %coup_h.1, ...), custom_call_target="tpu_custom_call" | custom-call | tf_op jit(solution)/shard_map/pallas_call | solution.py:682
  172.7 0.0 copy-start
  172.7 3.2 %copy.17 = f32[128,32,128]{2,1,0:T(8,128)} copy(f32[128,32,128]{2,1,0:T(8,128)} %bitcast.8) | data formatting | bytes 4194304
  176.0 0.0 copy-done
  176.0 1.3 copy.18
Async XLA Ops:
  172.7 3.2 %copy-start = (f32[4096,128]{1,0:T(8,128)S(1)}, f32[4096,128]{1,0:T(8,128)}, u32[]{:S(2)}) copy-start(f32[4096,128]{1,0:T(8,128)} %get-tuple-element.5) | copy-start | bytes 6291460

commit v3 on v2

--- a/solution.py
+++ b/solution.py
@@ -109,6 +109,18 @@
     return sine, sweep, meet, waves, gap
 
 
+def crossing(cols):
+    half = cols // 2
+    pick = np.zeros((16, 2 * cols), np.float32)
+    place = np.zeros((2, 16, cols), np.float32)
+    for row in range(2):
+        pick[2 * row, row * cols + half - 1] = 1.0
+        pick[2 * row + 1, row * cols + half] = 1.0
+        place[0, 2 * row + 1, row * half + half - 1] = 1.0
+        place[1, 2 * row, row * half] = 1.0
+    return pick.astype(BF16), place.astype(BF16)
+
+
 def tiled(plane):
     return plane.reshape(plane.shape[0] // 8, 8, plane.shape[1])
 
@@ -163,6 +175,8 @@
     meet_h,
     waves_h,
     gap_v,
+    pick_v,
+    place_v,
     sol_h,
     res_h,
     stage_g,
@@ -174,7 +188,9 @@
     waves_v,
     coup_v,
     u,
-    sb,
+    packed,
+    cross,
+    cross_in,
     r0,
     rh,
     strips,
@@ -210,7 +226,9 @@
     D2 = D // 2
     N = BLK
     cols = guess_h.shape[1]
-    WINDOW = min(4, D2 - 1)
+    H = cols // 2
+    lane = lax.broadcasted_iota(jnp.int32, (8, cols), 1)
+    lane1 = lane[:1]
     d = lax.axis_index("mode")
     s = lax.axis_index("slab")
     C = d // 2
@@ -280,7 +298,6 @@
     def take(x):
         plane = stage_g[pl.ds(x, N, stride=R), :]
         u[x + 1] = plane
-        sb[x + 1] = plane.astype(BF16)
 
     take(0)
     take(R - 1)
@@ -295,60 +312,73 @@
     coef_up.start()
     coef_down.start()
 
-    def pair_copies(it, i, g):
-        source = sb.at[pl.ds(2 * i, 2), pl.ds(g * HM, HM)]
-        for live, j, half in ((i < D2, 2 * i, 0), (i >= 1, 2 * i - 1, 1)):
-            target = strips.at[it, d, pl.ds(2 * half, 2), pl.ds(g * HM, HM)]
-            yield live, j, source, target
-
-    def send_pair(it, i, g):
-        for live, j, source, target in pair_copies(it, i, g):
-
-            @pl.when(jnp.logical_and(live, j != d))
+    def blend(first, second):
+        keep = lax.broadcasted_iota(jnp.int32, first.shape, 1) < H
+        return (
+            jnp.where(keep, first, pltpu.roll(second, H, 1)),
+            jnp.where(keep, pltpu.roll(first, H, 1), second),
+        )
+
+    def tile_copies(it, c, h, g):
+        j = 2 * c + h
+        half = pl.ds(g * HM, HM)
+        yield packed.at[c, h, :, half], strips.at[it, d, :, half], fs.at[it, g, j], fr.at[it, g, d]
+        if g == 1:
+            yield cross.at[c], cross_in.at[it, d], ps.at[it, j], pr.at[it, d]
+
+    def send_tiles(it, c, g):
+        half = pl.ds(g * HM, HM)
+        rows4 = [u[2 * c + n, half, :] for n in range(4)]
+        for n, (one, two) in enumerate(((1, 2), (0, 3))):
+            for h, plane in enumerate(blend(rows4[one], rows4[two])):
+                packed[c, h, n, half, :] = plane.astype(BF16)
+        if g == 1:
+            both = jnp.concatenate([u[2 * c + 1], u[2 * c + 2]], 1).astype(BF16)
+            cross[c] = lax.dot_general(
+                pick_v[...], both, (((1,), (1,)), ((), ())), preferred_element_type=F32
+            ).astype(BF16)
+        for h in range(2):
+            j = 2 * c + h
+
+            @pl.when(j != d)
             def _():
-                remote(source, target, fs.at[it, g, j], fr.at[it, g, d], j, s).start()
-
-            @pl.when(jnp.logical_and(live, j == d))
+                for source, target, send, recv in tile_copies(it, c, h, g):
+                    remote(source, target, send, recv, j, s).start()
+
+            @pl.when(j == d)
             def _():
-                pltpu.make_async_copy(source, target, fr.at[it, g, d]).start()
-
-    def sent_pairs(it):
+                for source, target, send, recv in tile_copies(it, c, h, g):
+                    pltpu.make_async_copy(source, target, recv).start()
+
+    def sent_tiles(it):
         @pl.loop(1, D)
         def _(t):
             j = (d + t) % D
             for g in range(2):
-                source = sb.at[pl.ds(0, 2), pl.ds(g * HM, HM)]
-                target = strips.at[it, d, pl.ds(0, 2), pl.ds(g * HM, HM)]
-                remote(source, target, fs.at[it, g, j], fr.at[it, g, d], j, s).wait_send()
-
-    def pair_at(it, k):
-        return 1 + (C + D2 - 2 + k) % (D2 - 1) if it == 0 else (C + k) % (D2 + 1)
-
-    def pairs(it):
-        return D2 - 1 if it == 0 else D2 + 1
-
-    def take_pair(k):
-        i = pair_at(0, k)
+                for source, target, send, recv in tile_copies(it, j // 2, j % 2, g):
+                    remote(source, target, send, recv, j, s).wait_send()
+
+    @pl.loop(0, D2)
+    def _(k):
+        x = 2 * ((C + k) % D2)
         for h in range(2):
-            x = 2 * i + h - 1
-
-            @pl.when(jnp.logical_and(x != 0, x != R - 1))
+
+            @pl.when(jnp.logical_and(x + h != 0, x + h != R - 1))
             def _():
-                take(x)
-
-    @pl.loop(0, WINDOW)
+                take(x + h)
+
+    @pl.loop(0, D2)
     def _(k):
-        take_pair(k)
-        for g in range(2):
-            send_pair(0, pair_at(0, k), g)
+        c = (C + k) % D2
+
+        @pl.when(jnp.logical_and(c != 0, c != D2 - 1))
+        def _():
+            for g in range(2):
+                send_tiles(0, c, g)
 
     load_b.start()
     for copy in table_loads:
         copy.start()
-
-    @pl.loop(WINDOW, D2 - 1)
-    def _(k):
-        take_pair(k)
 
     coef_up.wait()
     coef_down.wait()
@@ -364,22 +394,36 @@
     bottom = jnp.where(s == NS - 1, jnp.zeros((N, cols), F32), u[R + 1])
     u[0] = top
     u[R + 1] = bottom
-    sb[0] = top.astype(BF16)
-    sb[R + 1] = bottom.astype(BF16)
-    for g in range(2):
-        send_pair(0, 0, g)
-        send_pair(0, D2, g)
+    for c in (0, D2 - 1):
+        for g in range(2):
+            send_tiles(0, c, g)
 
     for n, value in enumerate(
         averages(cpad[0, pl.ds(8, R), :], cpad[0, pl.ds(7, R), :], cpad[0, pl.ds(9, R), :])
     ):
         mco[n] = jnp.broadcast_to(value[:, None, :], (R, 8, cols))
     for f in range(FIELDS):
-        rows3 = [
-            jnp.broadcast_to(cpad[f + 1, pl.ds(7 + d + n, 1), :], (8, cols)) for n in range(3)
-        ]
-        for n, value in enumerate(averages(rows3[1], rows3[0], rows3[2])):
-            fco[f, n] = value
+        near = [cpad[f + 1, pl.ds(7 + 2 * C + n, 1), :] for n in range(4)]
+        rows2 = [averages(near[n + 1], near[n], near[n + 2]) for n in range(2)]
+        total, left, right, up, down = (
+            jnp.where(p == 0, *blend(one, two)) for one, two in zip(*rows2)
+        )
+        zero = jnp.zeros_like(total)
+        at_left = lane1 % H == 0
+        at_right = lane1 % H == H - 1
+        over = jnp.where(
+            p == 0, jnp.where(at_right, right, zero), jnp.where(at_left, left, zero)
+        )
+        values = (
+            total,
+            jnp.where(at_left, zero, left),
+            jnp.where(at_right, zero, right),
+            jnp.where(lane1 < H, up, down),
+            jnp.where(lane1 < H, down, up),
+            over,
+        )
+        for n, value in enumerate(values):
+            fco[f, n] = jnp.broadcast_to(value, (8, cols))
     load_b.wait()
     for copy in table_loads:
         copy.wait()
@@ -397,21 +441,27 @@
             r0[x, pl.ds(m, CH), :] = side - flat(total)
 
     def make_images(it, src):
+        edges = lax.dot_general(
+            cross_in[it, src], place_v[p], (((0,), (0,)), ((), ())), preferred_element_type=F32
+        )
         for m in range(0, N, CH):
-            up, mid, down = (
-                strips[it, src, p + n, pl.ds(m, CH), :].astype(F32) for n in range(3)
-            )
-            left = tiled(pltpu.roll(mid, 1, 1))
-            right = tiled(pltpu.roll(mid, cols - 1, 1))
-            up, mid, down = tiled(up), tiled(mid), tiled(down)
+            mid, far = (strips[it, src, n, pl.ds(m, CH), :].astype(F32) for n in range(2))
+            terms = [
+                tiled(term)
+                for term in (
+                    mid,
+                    pltpu.roll(mid, 1, 1),
+                    pltpu.roll(mid, cols - 1, 1),
+                    far,
+                    pltpu.roll(mid, H, 1),
+                    edges[m : m + CH],
+                )
+            ]
             for f in range(FIELDS):
-                value = flat(
-                    fco[f, 0] * mid
-                    - fco[f, 1] * left
-                    - fco[f, 2] * right
-                    - fco[f, 3] * up
-                    - fco[f, 4] * down
-                )
+                value = fco[f, 0] * terms[0]
+                for n in range(1, 6):
+                    value = value - fco[f, n] * terms[n]
+                value = flat(value)
                 hi = value.astype(BF16)
                 lo = (value - hi.astype(F32)).astype(BF16)
                 images[3 * src + f, pl.ds(m, CH), :cols] = hi
@@ -423,56 +473,27 @@
         def source_at(k, q):
             return 2 * ((C + D2 - k) % D2) + q
 
-        def relay(k, q):
-            src = source_at(k, q)
-            shared = strips.at[it, src, 1 + p]
-            return remote(shared, shared, ps.at[it, src], pr.at[it, src], partner, s)
-
         def arrive(k):
             for q in range(2):
                 src = source_at(k, q)
                 for g in range(2):
-                    landed(
-                        strips.at[it, src, pl.ds(2 * p, 2), pl.ds(g * HM, HM)], fr.at[it, g, src]
-                    )
-                relay(k, q).start()
-
-        def imagine(k):
-            for q in range(2):
-                relay(k, q).wait_recv()
+                    landed(strips.at[it, src, :, pl.ds(g * HM, HM)], fr.at[it, g, src])
+                landed(cross_in.at[it, src], pr.at[it, src])
+
+        @pl.loop(0, D2)
+        def _(k):
+            apply_mean(2 * k)
+            apply_mean(2 * k + 1)
+
+        @pl.loop(0, D2)
+        def _(k):
+            if it == 0:
+                load_coupling(k).start()
+            arrive(k)
             for q in range(2):
                 make_images(it, source_at(k, q))
 
-        def send_next(k):
-            @pl.when(k + WINDOW < pairs(it))
-            def _():
-                for g in range(2):
-                    send_pair(it, pair_at(it, k + WINDOW), g)
-
-            if it == 0:
-                load_coupling(k).start()
-
-        arrive(0)
-        send_next(0)
-        apply_mean(0)
-        apply_mean(1)
-
-        @pl.loop(1, D2)
-        def _(k):
-            arrive(k)
-            send_next(k)
-            imagine(k - 1)
-            apply_mean(2 * k)
-            apply_mean(2 * k + 1)
-
-        imagine(D2 - 1)
-
-        @pl.loop(0, D2)
-        def _(k):
-            for q in range(2):
-                relay(k, q).wait_send()
-
-        sent_pairs(it)
+        sent_tiles(it)
         if it == 0:
 
             @pl.loop(0, D2)
@@ -531,9 +552,10 @@
                 landed(inq.at[it, a + q], or_.at[it, 0, a + q])
                 landed(ins.at[it, a + q], or_.at[it, 1, a + q])
             parts = []
+            terms = blend(*(inq[it, a + q].astype(F32) * ins[it, a + q] for q in range(2)))
             for q in range(2):
                 x = a + q
-                plane = r0[x] - inq[it, x].astype(F32) * ins[it, x]
+                plane = r0[x] - terms[q]
                 if last:
                     stage_b[pl.ds(x, N, stride=R), :] = plane
                     rh[x + 1] = transform(plane, fore_v[:, pl.ds(0, 2 * cols)])[0]
@@ -647,13 +669,12 @@
                     for h in range(2):
                         x = 2 * i + h
                         wave = flat(tiled(low[half, :]) * waves_v[x]).astype(BF16)
-                        plane = u[x, half, :] + transform(rh[x, half, :], back_v[...], wave)[0]
-                        u[x, half, :] = plane
-                        sb[x, half, :] = plane.astype(BF16)
-
-                    @pl.when(k < WINDOW)
-                    def _():
-                        send_pair(it + 1, i, g)
+                        change = transform(rh[x, half, :], back_v[...], wave)[0]
+                        u[x, half, :] = u[x, half, :] + change
+
+                @pl.loop(0, D2)
+                def _(k):
+                    send_tiles(it + 1, (C + k) % D2, g)
 
         @pl.loop(1, NS)
         def _(t):
@@ -682,7 +703,7 @@
     sol, res = pl.pallas_call(
         functools.partial(body, D, NS, R),
         out_shape=(flat_shape, flat_shape),
-        in_specs=[smem, smem, hbm, hbm, vmem, vmem, hbm] + [hbm] * 5 + [vmem],
+        in_specs=[smem, smem, hbm, hbm, vmem, vmem, hbm] + [hbm] * 5 + [vmem] * 3,
         out_specs=(hbm, hbm),
         scratch_shapes=[
             pltpu.VMEM((modes * R, cols), F32),
@@ -694,10 +715,12 @@
             pltpu.VMEM(waves.shape[1:], F32),
             pltpu.VMEM((D, MAXC, N, N), BF16),
             pltpu.VMEM((R + 2, N, cols), F32),
-            pltpu.VMEM((R + 2, N, cols), BF16),
+            pltpu.VMEM((D // 2, 2, 2, N, cols), BF16),
+            pltpu.VMEM((D // 2, 16, N), BF16),
+            pltpu.VMEM((ITERS, D, 16, N), BF16),
             pltpu.VMEM((R, N, cols), F32),
             pltpu.VMEM((R + 2, N, cols), F32),
-            pltpu.VMEM((ITERS, D, 4, N, cols), BF16),
+            pltpu.VMEM((ITERS, D, 2, N, cols), BF16),
             pltpu.VMEM((FIELDS * D + 1, N, 2 * cols), BF16),
             pltpu.VMEM((ITERS, D, N, cols), jnp.int16),
             pltpu.VMEM((ITERS, D, 1, cols), F32),
@@ -710,7 +733,7 @@
             pltpu.VMEM((2, 8, cols), F32),
             pltpu.VMEM((FIELDS + 1, R + 16, cols), F32),
             pltpu.VMEM((5, R, 8, cols), F32),
-            pltpu.VMEM((FIELDS, 5, 8, cols), F32),
+            pltpu.VMEM((FIELDS, 6, 8, cols), F32),
             sems((5,)),
             sems((4,)),
             sems((4,)),
@@ -739,7 +762,7 @@
         mean_coef,
         field_coef,
         coupling,
-        *(jnp.asarray(table) for table in (fore, back, sweep, meet, waves, gap)),
+        *(jnp.asarray(table) for table in (fore, back, sweep, meet, waves, gap, *crossing(cols))),
     )
     return sol.reshape(guess.shape), res.reshape(guess.shape)
 

time: 178 us -> 158 us (0.89)
  Pallas kernels: 172 us -> 153 us
    pallas_call x1, Pallas kernels: 172 us -> 153 us  [local(): pl.pallas_call(functools.partial(body, D, NS, R), out_shape=(flat_shape,...]
where the time goes in v3:
time: 158 us
  Pallas kernels  153 us (97%)
  local copies, waits for them, and re-layouts  4.55 us (3%)
    pallas_call x1, Pallas kernels, local(): pl.pallas_call(functools.partial(body, D, NS, R), out_shape=(flat_shape,...  153 us
    unnamed x4, local copies, waits for them, and re-layouts  4.55 us

profile of v3, /device:TPU:1, one launch (start us, length us, event | category | flops | bytes accessed | tf_op | source)
XLA Modules:
  0.0 157.8 jit_solution(12929661842247327797)
XLA Ops:
  0.6 152.6 %shard_map.158 = (f32[4096,128]{1,0:T(8,128)}, f32[4096,128]{1,0:T(8,128)}) custom-call(s32[16,32]{1,0:T(8,128)} %bitcast.9, s32[32]{0:T(128)} %count_s.1, f32[4096,128]{1,0:T(8,128)} %bitcast.5, f32[4096,128]{1,0:T(8,128)} %bitcast.6, f32[32,128]{1,0:T(8,128)} %mean_v.1, f32[3,32,128]{2,1,0:T(8,128)} %field_v.1, bf16[32,16,128,128]{3,2,1,0:T(8,128)(2,1)} %coup_h.1, ...), custom_call_target="tpu_custom_call" | custom-call | tf_op jit(solution)/shard_map/pallas_call | solution.py:703
  153.2 0.0 copy-start
  153.2 3.2 %copy.19 = f32[128,32,128]{2,1,0:T(8,128)} copy(f32[128,32,128]{2,1,0:T(8,128)} %bitcast.8) | data formatting | bytes 4194304
  156.4 0.0 copy-done
  156.4 1.3 copy.20
Async XLA Ops:
  153.2 3.2 %copy-start = (f32[4096,128]{1,0:T(8,128)S(1)}, f32[4096,128]{1,0:T(8,128)}, u32[]{:S(2)}) copy-start(f32[4096,128]{1,0:T(8,128)} %get-tuple-element.5) | copy-start | bytes 6291460

commit v4 on v2

--- a/solution.py
+++ b/solution.py
@@ -210,7 +210,6 @@
     D2 = D // 2
     N = BLK
     cols = guess_h.shape[1]
-    WINDOW = min(4, D2 - 1)
     d = lax.axis_index("mode")
     s = lax.axis_index("slab")
     C = d // 2
@@ -282,8 +281,11 @@
         u[x + 1] = plane
         sb[x + 1] = plane.astype(BF16)
 
-    take(0)
-    take(R - 1)
+    @pl.loop(0, D2)
+    def _(k):
+        take(2 * k)
+        take(2 * k + 1)
+
     pl.semaphore_wait(barrier, D - 1 + NS - 1)
 
     halo_up = remote(u.at[1], u.at[R + 1], hs.at[0], hr.at[0], d, above)
@@ -321,34 +323,14 @@
                 target = strips.at[it, d, pl.ds(0, 2), pl.ds(g * HM, HM)]
                 remote(source, target, fs.at[it, g, j], fr.at[it, g, d], j, s).wait_send()
 
-    def pair_at(it, k):
-        return 1 + (C + D2 - 2 + k) % (D2 - 1) if it == 0 else (C + k) % (D2 + 1)
-
-    def pairs(it):
-        return D2 - 1 if it == 0 else D2 + 1
-
-    def take_pair(k):
-        i = pair_at(0, k)
-        for h in range(2):
-            x = 2 * i + h - 1
-
-            @pl.when(jnp.logical_and(x != 0, x != R - 1))
-            def _():
-                take(x)
-
-    @pl.loop(0, WINDOW)
+    @pl.loop(0, D2 - 1)
     def _(k):
-        take_pair(k)
         for g in range(2):
-            send_pair(0, pair_at(0, k), g)
+            send_pair(0, 1 + (C + D2 - 2 + k) % (D2 - 1), g)
 
     load_b.start()
     for copy in table_loads:
         copy.start()
-
-    @pl.loop(WINDOW, D2 - 1)
-    def _(k):
-        take_pair(k)
 
     coef_up.wait()
     coef_down.wait()
@@ -443,27 +425,22 @@
             for q in range(2):
                 make_images(it, source_at(k, q))
 
-        def send_next(k):
-            @pl.when(k + WINDOW < pairs(it))
-            def _():
-                for g in range(2):
-                    send_pair(it, pair_at(it, k + WINDOW), g)
-
+        @pl.loop(0, D2)
+        def _(k):
+            apply_mean(2 * k)
+            apply_mean(2 * k + 1)
+
+        def load_some(k):
             if it == 0:
                 load_coupling(k).start()
 
         arrive(0)
-        send_next(0)
-        apply_mean(0)
-        apply_mean(1)
-
+        load_some(0)
         @pl.loop(1, D2)
         def _(k):
             arrive(k)
-            send_next(k)
+            load_some(k)
             imagine(k - 1)
-            apply_mean(2 * k)
-            apply_mean(2 * k + 1)
 
         imagine(D2 - 1)
 
@@ -559,10 +536,6 @@
         if not last:
             low_ex[s] = low[...].astype(BF16)
 
-            @pl.loop(1, NS)
-            def _(t):
-                swap_low(t).start()
-
         def swap(t, g):
             mine = ex.at[it, g, s]
             return remote(mine, mine, xs.at[it, g, t], xr.at[it, g, s], d, (s + t) % NS)
@@ -586,6 +559,8 @@
             @pl.loop(1, NS)
             def _(t):
                 swap(t, g).start()
+                if g == 0 and not last:
+                    swap_low(t).start()
 
         for g in range(2):
 
@@ -650,10 +625,7 @@
                         plane = u[x, half, :] + transform(rh[x, half, :], back_v[...], wave)[0]
                         u[x, half, :] = plane
                         sb[x, half, :] = plane.astype(BF16)
-
-                    @pl.when(k < WINDOW)
-                    def _():
-                        send_pair(it + 1, i, g)
+                    send_pair(it + 1, i, g)
 
         @pl.loop(1, NS)
         def _(t):

time: 178 us -> 149 us (0.84)
  Pallas kernels: 172 us -> 144 us
    pallas_call x1, Pallas kernels: 172 us -> 144 us  [local(): pl.pallas_call(functools.partial(body, D, NS, R), out_shape=(flat_shape,...]
where the time goes in v4:
time: 149 us
  Pallas kernels  144 us (97%)
  local copies, waits for them, and re-layouts  4.55 us (3%)
    pallas_call x1, Pallas kernels, local(): pl.pallas_call(functools.partial(body, D, NS, R), out_shape=(flat_shape,...  144 us
    unnamed x4, local copies, waits for them, and re-layouts  4.55 us

profile of v4, /device:TPU:1, one launch (start us, length us, event | category | flops | bytes accessed | tf_op | source)
XLA Modules:
  0.0 149.1 jit_solution(10705102744055801613)
XLA Ops:
  0.6 143.9 %shard_map.140 = (f32[4096,128]{1,0:T(8,128)}, f32[4096,128]{1,0:T(8,128)}) custom-call(s32[16,32]{1,0:T(8,128)} %bitcast.9, s32[32]{0:T(128)} %count_s.1, f32[4096,128]{1,0:T(8,128)} %bitcast.5, f32[4096,128]{1,0:T(8,128)} %bitcast.6, f32[32,128]{1,0:T(8,128)} %mean_v.1, f32[3,32,128]{2,1,0:T(8,128)} %field_v.1, bf16[32,16,128,128]{3,2,1,0:T(8,128)(2,1)} %coup_h.1, ...), custom_call_target="tpu_custom_call" | custom-call | tf_op jit(solution)/shard_map/pallas_call | solution.py:654
  144.6 0.0 copy-start
  144.6 3.2 %copy.17 = f32[128,32,128]{2,1,0:T(8,128)} copy(f32[128,32,128]{2,1,0:T(8,128)} %bitcast.8) | data formatting | bytes 4194304
  147.8 0.0 copy-done
  147.8 1.3 copy.18
Async XLA Ops:
  144.6 3.2 %copy-start = (f32[4096,128]{1,0:T(8,128)S(1)}, f32[4096,128]{1,0:T(8,128)}, u32[]{:S(2)}) copy-start(f32[4096,128]{1,0:T(8,128)} %get-tuple-element.5) | copy-start | bytes 6291460

commit v5 on v4

--- a/solution.py
+++ b/solution.py
@@ -444,12 +444,6 @@
 
         imagine(D2 - 1)
 
-        @pl.loop(0, D2)
-        def _(k):
-            for q in range(2):
-                relay(k, q).wait_send()
-
-        sent_pairs(it)
         if it == 0:
 
             @pl.loop(0, D2)
@@ -520,11 +514,6 @@
             if not last:
                 low[...] += flat(parts[0] + parts[1])
 
-        @pl.loop(1, D)
-        def _(t):
-            for copy in results((d + t) % D):
-                copy.wait_send()
-
         if last:
             store_r = pltpu.make_async_copy(stage_b, res_h, lsem.at[2])
             store_r.start()
@@ -561,6 +550,18 @@
                 swap(t, g).start()
                 if g == 0 and not last:
                     swap_low(t).start()
+
+        @pl.loop(0, D2)
+        def _(k):
+            for q in range(2):
+                relay(k, q).wait_send()
+
+        sent_pairs(it)
+
+        @pl.loop(1, D)
+        def _(t):
+            for copy in results((d + t) % D):
+                copy.wait_send()
 
         for g in range(2):
 

time: 149 us -> 148 us (level)
  Pallas kernels: 144 us -> 142 us
    pallas_call x1, Pallas kernels: 144 us -> 142 us  [local(): pl.pallas_call(functools.partial(body, D, NS, R), out_shape=(flat_shape,...]
where the time goes in v5:
time: 148 us; the launch traced here: 147 us
  Pallas kernels  142 us (96%)
  local copies, waits for them, and re-layouts  4.55 us (3%)
    pallas_call x1, Pallas kernels, local(): pl.pallas_call(functools.partial(body, D, NS, R), out_shape=(flat_shape,...  142 us
    unnamed x4, local copies, waits for them, and re-layouts  4.55 us

profile of v5, /device:TPU:1, one launch (start us, length us, event | category | flops | bytes accessed | tf_op | source)
XLA Modules:
  0.0 147.4 jit_solution(10782698694661612214)
XLA Ops:
  0.6 142.2 %shard_map.140 = (f32[4096,128]{1,0:T(8,128)}, f32[4096,128]{1,0:T(8,128)}) custom-call(s32[16,32]{1,0:T(8,128)} %bitcast.9, s32[32]{0:T(128)} %count_s.1, f32[4096,128]{1,0:T(8,128)} %bitcast.5, f32[4096,128]{1,0:T(8,128)} %bitcast.6, f32[32,128]{1,0:T(8,128)} %mean_v.1, f32[3,32,128]{2,1,0:T(8,128)} %field_v.1, bf16[32,16,128,128]{3,2,1,0:T(8,128)(2,1)} %coup_h.1, ...), custom_call_target="tpu_custom_call" | custom-call | tf_op jit(solution)/shard_map/pallas_call | solution.py:655
  142.9 0.0 copy-start
  142.9 3.2 %copy.17 = f32[128,32,128]{2,1,0:T(8,128)} copy(f32[128,32,128]{2,1,0:T(8,128)} %bitcast.8) | data formatting | bytes 4194304
  146.1 0.0 copy-done
  146.1 1.3 copy.18
Async XLA Ops:
  142.9 3.2 %copy-start = (f32[4096,128]{1,0:T(8,128)S(1)}, f32[4096,128]{1,0:T(8,128)}, u32[]{:S(2)}) copy-start(f32[4096,128]{1,0:T(8,128)} %get-tuple-element.5) | copy-start | bytes 6291460

commit v6 on v5

--- a/solution.py
+++ b/solution.py
@@ -297,10 +297,16 @@
     coef_up.start()
     coef_down.start()
 
+    def modes_of(it, g):
+        return pl.ds(g * HM, HM) if it else pl.ds(0, N)
+
+    def groups(it):
+        return range(2) if it else range(1)
+
     def pair_copies(it, i, g):
-        source = sb.at[pl.ds(2 * i, 2), pl.ds(g * HM, HM)]
+        source = sb.at[pl.ds(2 * i, 2), modes_of(it, g)]
         for live, j, half in ((i < D2, 2 * i, 0), (i >= 1, 2 * i - 1, 1)):
-            target = strips.at[it, d, pl.ds(2 * half, 2), pl.ds(g * HM, HM)]
+            target = strips.at[it, d, pl.ds(2 * half, 2), modes_of(it, g)]
             yield live, j, source, target
 
     def send_pair(it, i, g):
@@ -318,15 +324,14 @@
         @pl.loop(1, D)
         def _(t):
             j = (d + t) % D
-            for g in range(2):
-                source = sb.at[pl.ds(0, 2), pl.ds(g * HM, HM)]
-                target = strips.at[it, d, pl.ds(0, 2), pl.ds(g * HM, HM)]
+            for g in groups(it):
+                source = sb.at[pl.ds(0, 2), modes_of(it, g)]
+                target = strips.at[it, d, pl.ds(0, 2), modes_of(it, g)]
                 remote(source, target, fs.at[it, g, j], fr.at[it, g, d], j, s).wait_send()
 
     @pl.loop(0, D2 - 1)
     def _(k):
-        for g in range(2):
-            send_pair(0, 1 + (C + D2 - 2 + k) % (D2 - 1), g)
+        send_pair(0, 1 + (C + D2 - 2 + k) % (D2 - 1), 0)
 
     load_b.start()
     for copy in table_loads:
@@ -348,9 +353,8 @@
     u[R + 1] = bottom
     sb[0] = top.astype(BF16)
     sb[R + 1] = bottom.astype(BF16)
-    for g in range(2):
-        send_pair(0, 0, g)
-        send_pair(0, D2, g)
+    send_pair(0, 0, 0)
+    send_pair(0, D2, 0)
 
     for n, value in enumerate(
         averages(cpad[0, pl.ds(8, R), :], cpad[0, pl.ds(7, R), :], cpad[0, pl.ds(9, R), :])
@@ -413,10 +417,8 @@
         def arrive(k):
             for q in range(2):
                 src = source_at(k, q)
-                for g in range(2):
-                    landed(
-                        strips.at[it, src, pl.ds(2 * p, 2), pl.ds(g * HM, HM)], fr.at[it, g, src]
-                    )
+                for g in groups(it):
+                    landed(strips.at[it, src, pl.ds(2 * p, 2), modes_of(it, g)], fr.at[it, g, src])
                 relay(k, q).start()
 
         def imagine(k):

time: 148 us -> 147 us (level)
  no operation moved by 1% of the time
where the time goes in v6:
time: 147 us
  Pallas kernels  142 us (97%)
  local copies, waits for them, and re-layouts  4.55 us (3%)
    pallas_call x1, Pallas kernels, local(): pl.pallas_call(functools.partial(body, D, NS, R), out_shape=(flat_shape,...  142 us
    unnamed x4, local copies, waits for them, and re-layouts  4.55 us

profile of v6, /device:TPU:1, one launch (start us, length us, event | category | flops | bytes accessed | tf_op | source)
XLA Modules:
  0.0 146.9 jit_solution(13763110671130328237)
XLA Ops:
  0.6 141.7 %shard_map.140 = (f32[4096,128]{1,0:T(8,128)}, f32[4096,128]{1,0:T(8,128)}) custom-call(s32[16,32]{1,0:T(8,128)} %bitcast.9, s32[32]{0:T(128)} %count_s.1, f32[4096,128]{1,0:T(8,128)} %bitcast.5, f32[4096,128]{1,0:T(8,128)} %bitcast.6, f32[32,128]{1,0:T(8,128)} %mean_v.1, f32[3,32,128]{2,1,0:T(8,128)} %field_v.1, bf16[32,16,128,128]{3,2,1,0:T(8,128)(2,1)} %coup_h.1, ...), custom_call_target="tpu_custom_call" | custom-call | tf_op jit(solution)/shard_map/pallas_call | solution.py:657
  142.3 0.0 copy-start
  142.3 3.2 %copy.17 = f32[128,32,128]{2,1,0:T(8,128)} copy(f32[128,32,128]{2,1,0:T(8,128)} %bitcast.8) | data formatting | bytes 4194304
  145.6 0.0 copy-done
  145.6 1.3 copy.18
Async XLA Ops:
  142.3 3.2 %copy-start = (f32[4096,128]{1,0:T(8,128)S(1)}, f32[4096,128]{1,0:T(8,128)}, u32[]{:S(2)}) copy-start(f32[4096,128]{1,0:T(8,128)} %get-tuple-element.5) | copy-start | bytes 6291460
